TPU v7x, 128 devices: a whole 4x4x4 slice. The times are simulated.
128 devices in a mesh: grow: 8 (over x_lo, y), gcol: 16 (over z, x_hi, core).
Axes of the slice: x: 4 (x_hi: 2, x_lo: 2; x = x_hi * 2 + x_lo), y: 4, z: 4, core: 2. Of those that a mesh axis runs over, the one named last changes fastest.
Arguments:
- screened: bfloat16 [2, 16384, 16384], P(None, 'grow', 'gcol'), may hold values from -6 to 6
- elements: bfloat16 [2, 1024, 16384], P(None, None, ('grow', 'gcol')), may hold values from -0.046875 to 0.046875
- energy_grid: float32 [256], replicated, may hold values from -3 to 3
- band_index: int32 [256], replicated, may hold values from 0 to 255
- energy_index: int32 [4, 16], replicated, may hold values from 0 to 255
Outputs:
- sigma: float32 [2, 4, 16], replicated
All inputs are finite; a program needn't handle non-finite values.
Results may differ from a plain program's by a relative error of at most 0.0003.
Values may be sent and summed in bfloat16 or wider, within the bound.
No kernel may reach another device: no remote copies, remote signals or barrier semaphores. Data moves between devices by JAX's collectives and lax.ppermute only.
A program may use at most 128 MiB of HBM per device.

v0:
```python
import jax
import jax.numpy as jnp
from jax import lax
from jax.sharding import PartitionSpec as P


def spread(block, axis, source):
    block = jnp.where(lax.axis_index(axis) == source, block, jnp.zeros_like(block))
    return lax.psum(block, axis)


def weights(energy_grid, band_index, energy_index):
    points = lax.broadcasted_iota(jnp.int32, (1, energy_grid.shape[0]), 1)
    band_energy = jnp.sum(
        jnp.where(band_index[:, None] == points, energy_grid[None, :], 0.0), axis=-1
    )
    eval_energy = jnp.sum(
        jnp.where(energy_index[:, :, None] == points[None], energy_grid[None, None, :], 0.0),
        axis=-1,
    )
    offset = eval_energy[:, None, :] - band_energy[None, :, None]
    denom = offset * offset + 0.25
    return (offset / denom, -0.5 / denom)


def weigh(s_re, s_im, wre, wim):
    outer = wre.shape[0]
    summed = wre.shape[1]
    sre = s_re.reshape(outer, summed)[:, :, None]
    sim = s_im.reshape(outer, summed)[:, :, None]
    scale = summed ** (-0.5)
    out_re = scale * jnp.sum(wre * sre - wim * sim, axis=1)
    out_im = scale * jnp.sum(wre * sim + wim * sre, axis=1)
    return (out_re, out_im)


def local(screened, elements, energy_grid, band_index, energy_index):
    row_part = lax.all_gather(elements, "gcol", axis=2, tiled=True)
    ncol = screened.shape[2]
    place = lax.axis_index("gcol")
    half = lax.dynamic_slice_in_dim(row_part, place % 2 * ncol, ncol, 2)
    col_part = spread(half, "grow", place // 2)
    prod = jnp.einsum("mph,wgh->mpwg", col_part, screened, preferred_element_type=jnp.float32)
    yre = prod[0, :, 0] - prod[1, :, 1]
    yim = prod[1, :, 0] + prod[0, :, 1]
    rre = row_part[0].astype(jnp.float32)
    rim = row_part[1].astype(jnp.float32)
    s_re = jnp.sum(rre * yre + rim * yim, axis=-1)
    s_im = jnp.sum(rre * yim - rim * yre, axis=-1)
    wre, wim = weights(energy_grid, band_index, energy_index)
    total_re, total_im = lax.psum((s_re, s_im), ("grow", "gcol"))
    out_re, out_im = weigh(total_re, total_im, wre, wim)
    return jnp.stack([out_re, out_im])


def solution(mesh):
    in_specs = (P(None, "grow", "gcol"), P(None, None, ("grow", "gcol")), P(), P(), P())
    out_specs = P()
    return jax.shard_map(local, mesh=mesh, in_specs=in_specs, out_specs=out_specs, check_vma=False)
```

profile of v0, /device:TPU:0, one launch (start us, length us, event | category | flops | bytes accessed | tf_op | source)
XLA Modules:
  0.0 311.2 jit_solution(5005722360260161644)
XLA Ops:
  6.5 0.0 copy-start
  6.5 0.0 copy-start.1
  6.5 0.0 copy-start.2
  6.5 0.0 all-gather.2.cloned.1.call-start
  6.5 0.7 all-gather.2.cloned.1.call-update
  7.3 0.0 all-reduce.3.cloned.1.call-start
  7.3 82.1 %all-gather.2.cloned.1.call-done = bf16[2,1024,2048]{2,1,0:T(8,128)(2,1)} async-done(((bf16[2,1024,128]{2,1,0:T(8,128)(2,1)}), bf16[2,1024,2048]{2,1,0:T(8,128)(2,1)}) %all-gather.2.cloned.1.call-update) | async-done | bytes 8388624 | tf_op jit(solution)/shard_map/all_gather | solution.py:38
  89.5 5.4 %dynamic-slice_select_fusion = bf16[2,1024,1024]{2,1,0:T(8,128)(2,1)} fusion(bf16[2,1024,2048]{2,1,0:T(8,128)(2,1)} %all-gather.2.cloned.1.call-done, s32[]{:T(128)S(6)} %select_n.35, pred[]{:T(512)S(6)} %eq.37), kind=kLoop, calls=%fused_computation.17 | loop fusion | flops 2097152 | bytes 8388613 | tf_op jit(solution)/shard_map/jit(_where)/select_n | solution.py:8
  94.9 0.0 all-reduce.3.cloned.1.call-update
  94.9 0.0 copy-done
  94.9 0.0 copy-done.1
  94.9 0.2 select_reduce_fusion.1
  95.1 0.0 copy-done.2
  95.1 0.2 select_reduce_fusion
  95.2 102.5 %all-reduce.3.cloned.1.call-done = bf16[2,1024,1024]{2,1,0:T(8,128)(2,1)} async-done(((bf16[2,1024,1024]{2,1,0:T(8,128)(2,1)}), bf16[2,1024,1024]{2,1,0:T(8,128)(2,1)}) %all-reduce.3.cloned.1.call-update) | async-done | bytes 4194320 | tf_op jit(solution)/shard_map/psum | solution.py:9
  197.7 25.1 %fusion.6 = f32[2,1024,2,2048]{3,1,2,0:T(8,128)} fusion(bf16[2,2048,1024]{2,1,0:T(8,128)(2,1)} %param.5, bf16[2,1024,1024]{2,1,0:T(8,128)(2,1)} %all-reduce.3.cloned.1.call-done), kind=kOutput, calls=%fused_computation.12 | convolution fusion | flops 17179869184 | bytes 46137344 | tf_op jit(solution)/shard_map/mph,wgh->mpwg/dot_general | solution.py:43
  222.9 16.1 %fusion.1 = (f32[1024]{0:T(1024)S(1)}, f32[1024]{0:T(1024)S(1)}) fusion(bf16[2,1024,2048]{2,1,0:T(8,128)(2,1)} %all-gather.2.cloned.1.call-done, f32[2,1024,2,2048]{3,1,2,0:T(8,128)} %fusion.6), kind=kLoop, calls=%fused_computation.5 | loop fusion | flops 25163776 | bytes 41951232 | tf_op jit(solution)/shard_map/reduce_sum | solution.py:48
  239.0 64.6 %all-reduce = (f32[4,256]{1,0:T(4,128)S(1)}, f32[4,256]{1,0:T(4,128)S(1)}) all-reduce(f32[4,256]{1,0:T(4,128)S(1)} %mul.85, f32[4,256]{1,0:T(4,128)S(1)} %mul.80), channel_id=1, replica_groups=mesh['grow'=8,'gcol'=16] {'grow','gcol'}, use_global_device_ids=true, to_apply=%region_6.7 | all-reduce | flops 2048 | bytes 16384 | tf_op jit(solution)/shard_map/psum | solution.py:51
  303.6 0.2 subtract_reduce_fusion
  303.8 0.6 pad_maximum_fusion
  (3 shorter events, 0.0 us)
Async XLA Ops:
  6.5 88.3 %copy-start = (f32[256]{0:T(256)S(1)}, f32[256]{0:T(256)}, u32[]{:S(2)}) copy-start(f32[256]{0:T(256)} %param.7) | copy-start | bytes 3076
  6.5 88.4 %copy-start.1 = (s32[4,16]{1,0:T(4,128)S(1)}, s32[4,16]{1,0:T(4,128)}, u32[]{:S(2)}) copy-start(s32[4,16]{1,0:T(4,128)} %param.9) | copy-start | bytes 772
  6.5 88.5 %copy-start.2 = (s32[256]{0:T(256)S(1)}, s32[256]{0:T(256)}, u32[]{:S(2)}) copy-start(s32[256]{0:T(256)} %param.8) | copy-start | bytes 3076
  6.5 82.9 %all-gather.2.cloned.1.call-start = ((), (), s32[]{:S(2)}) async-start(), calls=%async_computation | async-start | bytes 8912896 | tf_op jit(solution)/shard_map/all_gather | solution.py:38
  7.3 190.5 %all-reduce.3.cloned.1.call-start = ((), (), s32[]{:S(2)}) async-start(), calls=%async_computation.1 | async-start | bytes 8388608 | tf_op jit(solution)/shard_map/psum | solution.py:9
Sparse Core Ops, SparseCore 0:
  9.7 79.7 all-gather.1
  95.0 102.7 all-reduce.2
where the time goes:
time: 312 us; the launch traced here: 311 us
  waiting for transfers between devices  185 us (59%)
  blocking collectives  64.6 us (21%)
  matrix products  25.1 us (8%)
  other arithmetic  22.6 us (7%)
  between operations  13.5 us (4%)
    psum x1, waiting for transfers between devices, spread(): return lax.psum(block, axis)  103 us
    all_gather x1, waiting for transfers between devices, local(): row_part = lax.all_gather(elements, 'gcol', axis=2, tiled=True)  82.1 us
    psum x1, blocking collectives, local(): total_re, total_im = lax.psum((s_re, s_im), ('grow', 'gcol'))  64.6 us
    dot_general x1, matrix products, local(): jnp.einsum('mph,wgh->mpwg', col_part, screened, preferred_element_type=jn...  25.1 us
    reduce_sum x1, other arithmetic, local(): s_re = jnp.sum(rre * yre + rim * yim, axis=-1)  16.1 us
  transfers between devices with their start and end apart: 2, of which 2 were waited for; matrix products, arithmetic and copies ran while one was open for 0% of the time, Pallas kernels for 0%

commit v1 on v0

v1 whole, which is shorter than its diff:
```python
import functools
import itertools

import jax
import jax.numpy as jnp
from jax import lax
from jax.experimental import pallas as pl
from jax.experimental.pallas import tpu as pltpu
from jax.sharding import Mesh
from jax.sharding import PartitionSpec as P

AXES = ("x_lo", "y", "z", "x_hi", "core")
ROW = ("x_lo", "y")
COL = ("z", "x_hi", "core")
STEP = 128
HALF = 512

MATCH = (
    (2, 0, 5, 7, 1, 3, 4, 6),
    (2, 3, 5, 4, 1, 0, 7, 6),
    (7, 4, 3, 1, 6, 5, 0, 2),
    (6, 7, 0, 2, 4, 5, 3, 1),
    (2, 0, 5, 4, 1, 3, 7, 6),
    (2, 0, 5, 4, 3, 1, 6, 7),
    (6, 4, 2, 1, 7, 5, 0, 3),
    (4, 6, 2, 0, 5, 7, 3, 1),
    (6, 4, 3, 1, 5, 7, 0, 2),
    (6, 7, 1, 0, 4, 5, 3, 2),
    (2, 0, 5, 6, 1, 3, 7, 4),
    (1, 3, 5, 4, 2, 0, 6, 7),
    (7, 6, 3, 1, 5, 4, 0, 2),
    (6, 7, 3, 1, 4, 5, 2, 0),
    (3, 0, 5, 7, 1, 2, 4, 6),
    (1, 3, 7, 5, 0, 2, 4, 6),
)


def pairs_of(move):
    found = []
    for x_lo, y, z, x_hi, core in itertools.product(range(2), range(4), range(4), range(2), range(2)):
        x, ny, nz, ncore = move(2 * x_hi + x_lo, y, z, core)
        x, ny, nz = x % 4, ny % 4, nz % 4
        source = (((x_lo * 4 + y) * 4 + z) * 2 + x_hi) * 2 + core
        found.append((source, (((x % 2 * 4 + ny) * 4 + nz) * 2 + x // 2) * 2 + ncore))
    return found


Z_UP = pairs_of(lambda x, y, z, c: (x, y, z + 1, c))
Z_DOWN = pairs_of(lambda x, y, z, c: (x, y, z - 1, c))
Z_ON = pairs_of(lambda x, y, z, c: (x, y, z + 1 - 2 * c, c))
Y_UP = pairs_of(lambda x, y, z, c: (x, y + 1, z, c))
Y_DOWN = pairs_of(lambda x, y, z, c: (x, y - 1, z, c))
Y_ON = pairs_of(lambda x, y, z, c: (x, y + 1 - 2 * c, z, c))
X_FAR = pairs_of(lambda x, y, z, c: (x + 2, y, z, c))
X_NEAR = pairs_of(lambda x, y, z, c: (x ^ 1, y, z, c))
CORE = pairs_of(lambda x, y, z, c: (x, y, z, 1 - c))
TURN = [(c // 2 * 16 + c % 2 * 8 + j, MATCH[c][j] * 16 + c) for c in range(16) for j in range(8)]
ROUNDS = (
    CORE,
    X_NEAR,
    pairs_of(lambda x, y, z, c: (x + (1 if x % 2 else -1), y, z, c)),
    pairs_of(lambda x, y, z, c: (x, y ^ 1, z, c)),
    pairs_of(lambda x, y, z, c: (x, y + (1 if y % 2 else -1), z, c)),
    pairs_of(lambda x, y, z, c: (x, y, z ^ 1, c)),
    pairs_of(lambda x, y, z, c: (x, y, z + (1 if z % 2 else -1), c)),
)


def send(block, pairs):
    return lax.ppermute(block, AXES, pairs)


def ring(block, up, down, on, core):
    below = send(block, up)
    above = send(block, down)
    far = send(jnp.where(core == 0, below, above), on)
    return [block, below, above, far]


def weights(energy_grid, band_index, energy_index):
    points = lax.broadcasted_iota(jnp.int32, (1, energy_grid.shape[0]), 1)
    band_energy = jnp.sum(
        jnp.where(band_index[:, None] == points, energy_grid[None, :], 0.0), axis=-1
    )
    eval_energy = jnp.sum(
        jnp.where(energy_index[:, :, None] == points[None], energy_grid[None, None, :], 0.0),
        axis=-1,
    )
    offset = eval_energy[:, None, :] - band_energy[None, :, None]
    denom = offset * offset + 0.25
    scale = band_index.shape[0] ** (-0.5)
    w = jnp.stack([offset / denom, -0.5 / denom]) * scale
    return w.reshape(2, -1, w.shape[-1])


def product_body(place, *refs):
    blocks, w_ref, z_ref, lhs = refs[:16], refs[16], refs[-2], refs[-1]

    @pl.when(pl.program_id(0) == 0)
    def _():
        for i, block in enumerate(blocks):
            at = pl.multiple_of(place[i] * STEP, STEP)
            late = pl.multiple_of(place[i] * STEP + 2048, STEP)
            re, im = block[0], block[1]
            lhs[:HALF, pl.ds(at, STEP)] = re
            lhs[:HALF, pl.ds(late, STEP)] = im
            lhs[HALF:, pl.ds(at, STEP)] = -im
            lhs[HALF:, pl.ds(late, STEP)] = re

    w = w_ref[...].reshape(4096, -1)
    for m in range(4):
        part = jnp.dot(lhs[m * 256 : m * 256 + 256, :], w, preferred_element_type=jnp.float32)
        z_ref[m // 2, m % 2 * 256 : m % 2 * 256 + 256, :] = part


def product(chunk, place, blocks, screened, z=None):
    width = 256
    specs = [pl.BlockSpec((2, HALF, STEP), lambda n, s: (0, chunk, 0))] * 16
    specs.append(pl.BlockSpec((2, 2048, width), lambda n, s: (0, 0, n)))
    args = [place, *blocks, screened]
    alias = {}
    if z is not None:
        specs.append(pl.BlockSpec(memory_space=pl.ANY))
        args.append(z)
        alias = {18: 0}
    return pl.pallas_call(
        product_body,
        out_shape=jax.ShapeDtypeStruct((2, 1024, 1024), jnp.float32),
        grid_spec=pltpu.PrefetchScalarGridSpec(
            num_scalar_prefetch=1,
            grid=(1024 // width,),
            in_specs=specs,
            out_specs=pl.BlockSpec((2, HALF, width), lambda n, s: (0, chunk, n)),
            scratch_shapes=[pltpu.VMEM((2 * HALF, 4096), jnp.bfloat16)],
        ),
        input_output_aliases=alias,
        compiler_params=pltpu.CompilerParams(vmem_limit_bytes=48 << 20),
        cost_estimate=pl.CostEstimate(flops=8 << 30, transcendentals=0, bytes_accessed=16 << 20),
    )(*args)


def form_body(place, *refs):
    blocks, z_ref, w_ref, out = refs[:8], refs[8], refs[9], refs[10]
    step = pl.program_id(0)

    @pl.when(step == 0)
    def _():
        out[...] = jnp.zeros_like(out)

    s_re = jnp.zeros((STEP, STEP), jnp.float32)
    s_im = jnp.zeros((STEP, STEP), jnp.float32)
    for i, block in enumerate(blocks):
        at = pl.multiple_of(place[i] * STEP, STEP)
        z_re, z_im = z_ref[0, :, pl.ds(at, STEP)], z_ref[1, :, pl.ds(at, STEP)]
        re, im = block[0].astype(jnp.float32), block[1].astype(jnp.float32)
        s_re += z_re * re - z_im * im
        s_im += z_re * im + z_im * re
    s_re = jnp.sum(s_re, axis=1, keepdims=True)
    s_im = jnp.sum(s_im, axis=1, keepdims=True)
    w_re, w_im = w_ref[0], w_ref[1]
    n = step // 2
    out[0, pl.ds(n, 1), :] += jnp.sum(w_re * s_re - w_im * s_im, axis=0, keepdims=True)
    out[1, pl.ds(n, 1), :] += jnp.sum(w_re * s_im + w_im * s_re, axis=0, keepdims=True)


def form(place, blocks, z, w):
    specs = [pl.BlockSpec((2, STEP, STEP), lambda i, s: (0, i, 0))] * 8
    specs.append(pl.BlockSpec((2, STEP, 1024), lambda i, s: (0, i, 0)))
    specs.append(pl.BlockSpec((2, STEP, 16), lambda i, s: (0, i, 0)))
    return pl.pallas_call(
        form_body,
        out_shape=jax.ShapeDtypeStruct((2, 4, 16), jnp.float32),
        grid_spec=pltpu.PrefetchScalarGridSpec(
            num_scalar_prefetch=1,
            grid=(8,),
            in_specs=specs,
            out_specs=pl.BlockSpec((2, 4, 16), lambda i, s: (0, 0, 0)),
        ),
        cost_estimate=pl.CostEstimate(flops=8 << 20, transcendentals=0, bytes_accessed=12 << 20),
    )(place, *blocks, z, w)


def local(screened, elements, energy_grid, band_index, energy_index):
    x_lo, y, z = lax.axis_index("x_lo"), lax.axis_index("y"), lax.axis_index("z")
    x_hi, core = lax.axis_index("x_hi"), lax.axis_index("core")
    w = weights(energy_grid, band_index, energy_index)

    turned = send(elements, TURN)
    across = send(elements, X_FAR)
    own = ring(elements, Z_UP, Z_DOWN, Z_ON, core) + ring(across, Z_UP, Z_DOWN, Z_ON, core)
    other = [send(block, CORE) for block in own]
    beside = send(turned, X_NEAR)
    columns = ring(turned, Y_UP, Y_DOWN, Y_ON, core) + ring(beside, Y_UP, Y_DOWN, Y_ON, core)

    back = jnp.array([0, 1, 3, 2], jnp.int32)
    layer = (z - back + 4) % 4
    chip = jnp.concatenate([layer * 2 + x_hi, layer * 2 + 1 - x_hi])
    row_place = jnp.concatenate([chip * 2 + core, chip * 2 + 1 - core])
    line = (y - back + 4) % 4
    source = jnp.concatenate([x_lo * 4 + line, (1 - x_lo) * 4 + line])
    taken = jnp.array(MATCH, jnp.int32)[(z * 2 + x_hi) * 2 + core]
    col_place = jnp.sum(jnp.where(source[:, None] == taken[None, :], jnp.arange(8, dtype=jnp.int32)[None, :], 0), axis=1)

    blocks = own + other
    zz = product(0, row_place, blocks, screened)
    zz = product(1, row_place, blocks, screened, zz)
    out = form(col_place, columns, zz, w)
    for pairs in ROUNDS:
        out = out + send(out, pairs)
    return out


def solution(mesh):
    split = Mesh(mesh.devices.reshape(2, 4, 4, 2, 2), AXES)
    in_specs = (P(None, ROW, COL), P(None, None, ROW + COL), P(), P(), P())
    return jax.shard_map(local, mesh=split, in_specs=in_specs, out_specs=P(), check_vma=False)
```

time: 312 us -> 151 us (0.48)
  waiting for transfers between devices: 185 us -> 37.9 us
  blocking collectives: 64.6 us -> 0 us
  starting transfers between devices: 0.04 us -> 53 us
  Pallas kernels: 0 us -> 40.6 us
  matrix products: 25.1 us -> 0 us
  between operations: 13.5 us -> 0.2 us
  other arithmetic: 22.6 us -> 10.1 us
  local copies, waits for them, and re-layouts: 0.03 us -> 8.72 us
    psum x1 -> x0, waiting for transfers between devices: 103 us -> none  [spread(): return lax.psum(block, axis)]
    all_gather x1 -> x0, waiting for transfers between devices: 82.1 us -> none  [local(): row_part = lax.all_gather(elements, 'gcol', axis=2, tiled=True)]
    psum x1 -> x0, blocking collectives: 64.6 us -> none  [local(): total_re, total_im = lax.psum((s_re, s_im), ('grow', 'gcol'))]
    ppermute x0 -> x30, starting transfers between devices: none -> 53 us  [send(): return lax.ppermute(block, AXES, pairs)]
    pallas_call x0 -> x3, Pallas kernels: none -> 40.6 us  [the longest x2 31.5 us: product(): pl.pallas_call(product_body, out_shape=jax.ShapeDtypeStruct((2, 1024, 102...]
    ppermute x0 -> x30, waiting for transfers between devices: none -> 37.9 us  [send(): return lax.ppermute(block, AXES, pairs)]
    dot_general x1 -> x0, matrix products: 25.1 us -> none  [local(): jnp.einsum('mph,wgh->mpwg', col_part, screened, preferred_element_type=jn...]
    reduce_sum x2 -> x1, other arithmetic: 16.3 us -> 0.68 us  [local(): jnp.sum(jnp.where(source[:, None] == taken[None, :], jnp.arange(8, dtype=...]
  transfers between devices with their start and end apart: 2 -> 30, of which waited for: 2 -> 12; matrix products, arithmetic and copies ran while one was open for 0% -> 7% of each run, Pallas kernels for 0% -> 21%
where the time goes in v1:
time: 151 us; the launch traced here: 150 us
  starting transfers between devices  53 us (35%)
  Pallas kernels  40.6 us (27%)
  waiting for transfers between devices  37.9 us (25%)
  other arithmetic  10.1 us (7%)
  local copies, waits for them, and re-layouts  8.72 us (6%)
    ppermute x30, starting transfers between devices, send(): return lax.ppermute(block, AXES, pairs)  53 us
    ppermute x30, waiting for transfers between devices, send(): return lax.ppermute(block, AXES, pairs)  37.9 us
    pallas_call x2, Pallas kernels, product(): pl.pallas_call(product_body, out_shape=jax.ShapeDtypeStruct((2, 1024, 102...  31.5 us
    pallas_call x1, Pallas kernels, form(): pl.pallas_call(form_body, out_shape=jax.ShapeDtypeStruct((2, 4, 16), jnp....  9.05 us
    unnamed x26, local copies, waits for them, and re-layouts  6.47 us
    select_n x4, other arithmetic, ring(): far = send(jnp.where(core == 0, below, above), on)  3.14 us
  transfers between devices with their start and end apart: 30, of which 12 were waited for; matrix products, arithmetic and copies ran while one was open for 7% of the time, Pallas kernels for 21%

profile of v1, /device:TPU:0, one launch (start us, length us, event | category | flops | bytes accessed | tf_op | source)
XLA Modules:
  0.0 150.5 jit_solution(8448324213551107968)
XLA Ops:
  0.0 3.1 %collective-permute-start.11 = (bf16[2,1024,128]{2,1,0:T(8,128)(2,1)}, bf16[2,1024,128]{2,1,0:T(8,128)(2,1)S(1)}, u32[]{:S(2)}, u32[]{:S(2)}) collective-permute-start(bf16[2,1024,128]{2,1,0:T(8,128)(2,1)} %refs_0_.3), channel_id=1, source_target_pairs={{0,2},{1,3},{2,0},{3,1},{4,6},{5,7},{6,4},{7,5},{8,10},{9,11},{10,... | collective-permute-start | bytes 1572872 | tf_op jit(solution)/shard_map/ppermute | solution.py:70
  3.1 1.9 %collective-permute-start.8 = (bf16[2,1024,128]{2,1,0:T(8,128)(2,1)}, bf16[2,1024,128]{2,1,0:T(8,128)(2,1)S(1)}, u32[]{:S(2)}, u32[]{:S(2)}) collective-permute-start(bf16[2,1024,128]{2,1,0:T(8,128)(2,1)} %refs_0_.3), channel_id=1, source_target_pairs={{0,4},{1,5},{2,6},{3,7},{4,8},{5,9},{6,10},{7,11},{8,12},{9,13},{1... | collective-permute-start | bytes 1572872 | tf_op jit(solution)/shard_map/ppermute | solution.py:70
  5.0 2.1 %collective-permute-start.9 = (bf16[2,1024,128]{2,1,0:T(8,128)(2,1)}, bf16[2,1024,128]{2,1,0:T(8,128)(2,1)S(1)}, u32[]{:S(2)}, u32[]{:S(2)}) collective-permute-start(bf16[2,1024,128]{2,1,0:T(8,128)(2,1)} %refs_0_.3), channel_id=1, source_target_pairs={{0,12},{1,13},{2,14},{3,15},{4,0},{5,1},{6,2},{7,3},{8,4},{9,5},{1... | collective-permute-start | bytes 1572872 | tf_op jit(solution)/shard_map/ppermute | solution.py:70
  7.2 3.2 %collective-permute-start = (bf16[2,1024,128]{2,1,0:T(8,128)(2,1)}, bf16[2,1024,128]{2,1,0:T(8,128)(2,1)}, u32[]{:S(2)}, u32[]{:S(2)}) collective-permute-start(bf16[2,1024,128]{2,1,0:T(8,128)(2,1)} %refs_0_.3), channel_id=1, source_target_pairs={{0,32},{1,0},{2,80},{3,112},{4,16},{5,48},{6,64},{7,96},{8,33},{9,... | collective-permute-start | bytes 1572872 | tf_op jit(solution)/shard_map/ppermute | solution.py:70
  10.3 0.7 broadcast_add_fusion.1
  11.0 0.9 select_reduce_fusion
  11.9 3.5 %collective-permute-done.11.refs_4_ = bf16[2,1024,128]{2,1,0:T(8,128)(2,1)S(1)} collective-permute-done((bf16[2,1024,128]{2,1,0:T(8,128)(2,1)}, bf16[2,1024,128]{2,1,0:T(8,128)(2,1)S(1)}, u32[]{:S(2)}, u32[]{:S(2)}) %collective-permute-start.11) | collective-permute-done | bytes 524320 | tf_op jit(solution)/shard_map/ppermute | solution.py:70
  15.4 2.1 %collective-permute-start.12 = (bf16[2,1024,128]{2,1,0:T(8,128)(2,1)S(1)}, bf16[2,1024,128]{2,1,0:T(8,128)(2,1)S(1)}, u32[]{:S(2)}, u32[]{:S(2)}) collective-permute-start(bf16[2,1024,128]{2,1,0:T(8,128)(2,1)S(1)} %collective-permute-done.11.refs_4_), channel_id=1, source_target_pairs={{0,4},{1,5},{2,6},{3,7},{4,8},{5,9},{6,10},{7,11},{8,12},{9,13},{1... | collective-permute-start | bytes 1572872 | tf_op jit(solution)/shard_map/ppermute | solution.py:70
  17.5 2.1 %collective-permute-start.13 = (bf16[2,1024,128]{2,1,0:T(8,128)(2,1)S(1)}, bf16[2,1024,128]{2,1,0:T(8,128)(2,1)S(1)}, u32[]{:S(2)}, u32[]{:S(2)}) collective-permute-start(bf16[2,1024,128]{2,1,0:T(8,128)(2,1)S(1)} %collective-permute-done.11.refs_4_), channel_id=1, source_target_pairs={{0,12},{1,13},{2,14},{3,15},{4,0},{5,1},{6,2},{7,3},{8,4},{9,5},{1... | collective-permute-start | bytes 1572872 | tf_op jit(solution)/shard_map/ppermute | solution.py:70
  19.6 0.8 select_reduce_fusion.1
  20.5 0.1 copy.12
  20.5 0.1 sub.62
  20.7 2.6 %collective-permute-done.8.refs_1_ = bf16[2,1024,128]{2,1,0:T(8,128)(2,1)S(1)} collective-permute-done((bf16[2,1024,128]{2,1,0:T(8,128)(2,1)}, bf16[2,1024,128]{2,1,0:T(8,128)(2,1)S(1)}, u32[]{:S(2)}, u32[]{:S(2)}) %collective-permute-start.8) | collective-permute-done | bytes 524320 | tf_op jit(solution)/shard_map/ppermute | solution.py:70
  23.4 4.4 %collective-permute-start.10 = (bf16[2,1024,128]{2,1,0:T(8,128)(2,1)S(1)}, bf16[2,1024,128]{2,1,0:T(8,128)(2,1)S(1)}, u32[]{:S(2)}, u32[]{:S(2)}) collective-permute-start(bf16[2,1024,128]{2,1,0:T(8,128)(2,1)S(1)} %broadcast_select_fusion.1), channel_id=1, source_target_pairs={{0,4},{1,13},{2,6},{3,15},{4,8},{5,1},{6,10},{7,3},{8,12},{9,5},{1... | collective-permute-start | bytes 1572872 | tf_op jit(solution)/shard_map/ppermute | solution.py:70
  27.8 0.4 collective-permute-start.19
  28.2 4.8 %collective-permute-done.12.refs_5_ = bf16[2,1024,128]{2,1,0:T(8,128)(2,1)S(1)} collective-permute-done((bf16[2,1024,128]{2,1,0:T(8,128)(2,1)S(1)}, bf16[2,1024,128]{2,1,0:T(8,128)(2,1)S(1)}, u32[]{:S(2)}, u32[]{:S(2)}) %collective-permute-start.12) | collective-permute-done | bytes 524320 | tf_op jit(solution)/shard_map/ppermute | solution.py:70
  33.0 6.4 %collective-permute-start.16 = (bf16[2,1024,128]{2,1,0:T(8,128)(2,1)S(1)}, bf16[2,1024,128]{2,1,0:T(8,128)(2,1)S(1)}, u32[]{:S(2)}, u32[]{:S(2)}) collective-permute-start(bf16[2,1024,128]{2,1,0:T(8,128)(2,1)S(1)} %collective-permute-done.8.refs_1_), channel_id=1, source_target_pairs={{0,1},{1,0},{2,3},{3,2},{4,5},{5,4},{6,7},{7,6},{8,9},{9,8},{10,11... | collective-permute-start | bytes 1572872 | tf_op jit(solution)/shard_map/ppermute | solution.py:70
  39.4 3.7 %collective-permute-start.4 = (bf16[2,1024,128]{2,1,0:T(8,128)(2,1)}, bf16[2,1024,128]{2,1,0:T(8,128)(2,1)}, u32[]{:S(2)}, u32[]{:S(2)}) collective-permute-start(bf16[2,1024,128]{2,1,0:T(8,128)(2,1)} %collective-permute-done.refs_0_), channel_id=1, source_target_pairs={{0,64},{1,65},{2,66},{3,67},{4,68},{5,69},{6,70},{7,71},{8,72},{9,... | collective-permute-start | bytes 1572872 | tf_op jit(solution)/shard_map/ppermute | solution.py:70
  43.2 0.1 broadcast_add_fusion
  43.2 0.1 pad_add_fusion.1.place
  43.3 0.9 broadcast_select_fusion
  44.2 0.8 copy-done.1
  45.0 3.2 %collective-permute-start.2 = (bf16[2,1024,128]{2,1,0:T(8,128)(2,1)}, bf16[2,1024,128]{2,1,0:T(8,128)(2,1)}, u32[]{:S(2)}, u32[]{:S(2)}) collective-permute-start(bf16[2,1024,128]{2,1,0:T(8,128)(2,1)} %collective-permute-done.refs_0_), channel_id=1, source_target_pairs={{0,48},{1,49},{2,50},{3,51},{4,52},{5,53},{6,54},{7,55},{8,56},{9,... | collective-permute-start | bytes 1572872 | tf_op jit(solution)/shard_map/ppermute | solution.py:70
  48.3 1.6 %collective-permute-start.14 = (bf16[2,1024,128]{2,1,0:T(8,128)(2,1)}, bf16[2,1024,128]{2,1,0:T(8,128)(2,1)}, u32[]{:S(2)}, u32[]{:S(2)}) collective-permute-start(bf16[2,1024,128]{2,1,0:T(8,128)(2,1)} %broadcast_select_fusion), channel_id=1, source_target_pairs={{0,4},{1,13},{2,6},{3,15},{4,8},{5,1},{6,10},{7,3},{8,12},{9,5},{1... | collective-permute-start | bytes 1572872 | tf_op jit(solution)/shard_map/ppermute | solution.py:70
  49.9 4.8 %collective-permute-done.4.refs_4_ = bf16[2,1024,128]{2,1,0:T(8,128)(2,1)} collective-permute-done((bf16[2,1024,128]{2,1,0:T(8,128)(2,1)}, bf16[2,1024,128]{2,1,0:T(8,128)(2,1)}, u32[]{:S(2)}, u32[]{:S(2)}) %collective-permute-start.4) | collective-permute-done | bytes 524320 | tf_op jit(solution)/shard_map/ppermute | solution.py:70
  54.8 0.8 copy-done.5
  55.5 3.2 %collective-permute-start.6 = (bf16[2,1024,128]{2,1,0:T(8,128)(2,1)}, bf16[2,1024,128]{2,1,0:T(8,128)(2,1)}, u32[]{:S(2)}, u32[]{:S(2)}) collective-permute-start(bf16[2,1024,128]{2,1,0:T(8,128)(2,1)} %collective-permute-done.4.refs_4_), channel_id=1, source_target_pairs={{0,48},{1,49},{2,50},{3,51},{4,52},{5,53},{6,54},{7,55},{8,56},{9,... | collective-permute-start | bytes 1572872 | tf_op jit(solution)/shard_map/ppermute | solution.py:70
  58.8 1.4 copy.13
  60.2 0.7 dynamic-slice_bitcast_fusion
  60.9 0.7 select_reduce_fusion.2.place
  61.6 2.3 %broadcast_multiply_fusion.refs_9_ = f32[2,1024,16]{2,1,0:T(8,128)} fusion(f32[2,1024,16]{2,1,0:T(8,128)} %copy.13), kind=kLoop, calls=%fused_computation | loop fusion | flops 32768 | bytes 262144 | tf_op jit(solution)/shard_map/mul | solution.py:92
  63.9 0.5 collective-permute-start.20
  64.4 0.1 collective-permute-start.21
  64.5 6.0 %collective-permute-done.5.refs_5_ = bf16[2,1024,128]{2,1,0:T(8,128)(2,1)} collective-permute-done((bf16[2,1024,128]{2,1,0:T(8,128)(2,1)}, bf16[2,1024,128]{2,1,0:T(8,128)(2,1)}, u32[]{:S(2)}, u32[]{:S(2)}) %collective-permute-start.5) | collective-permute-done | bytes 524320 | tf_op jit(solution)/shard_map/ppermute | solution.py:70
  70.5 0.5 collective-permute-start.22
  71.0 1.1 broadcast_select_fusion.3
  72.1 1.1 broadcast_select_fusion.2
  73.2 0.1 collective-permute-start.3
  73.3 0.9 collective-permute-start.7
  74.3 0.7 copy-done.8
  75.0 0.2 copy-done.9
  75.2 0.8 copy-done.11
  76.0 1.0 copy-done.2
  77.1 1.0 copy-done.4
  78.1 1.0 copy-done.6
  79.2 15.8 %shard_map.73.refs_17_ = f32[2,1024,1024]{2,1,0:T(8,128)} custom-call(s32[16]{0:T(128)S(1)} %pad_add_fusion.1.place, bf16[2,1024,128]{2,1,0:T(8,128)(2,1)S(1)} %copy-done, bf16[2,1024,128]{2,1,0:T(8,128)(2,1)S(1)} %collective-permute-done.8.refs_1_, bf16[2,1024,128]{2,1,0:T(8,128)(2,1)S(1)} %collective-permute-done.9.refs_2_, ...), custom_call_target="tpu_custom_call" | custom-call | flops 8589934592 | bytes 16777216 | tf_op jit(solution)/shard_map/pallas_call | solution.py:126
  94.9 15.7 %shard_map.74.refs_8_ = f32[2,1024,1024]{2,1,0:T(8,128)} custom-call(s32[16]{0:T(128)S(1)} %pad_add_fusion.1.place, bf16[2,1024,128]{2,1,0:T(8,128)(2,1)S(1)} %copy-done, bf16[2,1024,128]{2,1,0:T(8,128)(2,1)S(1)} %collective-permute-done.8.refs_1_, bf16[2,1024,128]{2,1,0:T(8,128)(2,1)S(1)} %collective-permute-done.9.refs_2_, ...), custom_call_target="tpu_custom_call", output_to_operand_aliasing={{}: (18, {})} | custom-call | flops 8589934592 | bytes 16777216 | tf_op jit(solution)/shard_map/pallas_call | solution.py:126
  110.7 9.1 %shard_map.75 = f32[2,4,16]{2,1,0:T(4,128)} custom-call(s32[8]{0:T(128)} %select_reduce_fusion.2.place, bf16[2,1024,128]{2,1,0:T(8,128)(2,1)} %collective-permute-done.refs_0_, bf16[2,1024,128]{2,1,0:T(8,128)(2,1)} %collective-permute-done.1.refs_1_, bf16[2,1024,128]{2,1,0:T(8,128)(2,1)} %collective-permute-done.2.refs_2_, ...), custom_call_target="tpu_custom_call" | custom-call | flops 8388608 | bytes 12582912 | tf_op jit(solution)/shard_map/pallas_call | solution.py:170
  119.7 2.0 %collective-permute-start.23 = (f32[2,4,16]{2,1,0:T(4,128)}, f32[2,4,16]{2,1,0:T(4,128)S(1)}, u32[]{:S(2)}, u32[]{:S(2)}) collective-permute-start(f32[2,4,16]{2,1,0:T(4,128)} %shard_map.75), channel_id=1, source_target_pairs={{0,1},{1,0},{2,3},{3,2},{4,5},{5,4},{6,7},{7,6},{8,9},{9,8},{10,11... | collective-permute-start | bytes 1544 | tf_op jit(solution)/shard_map/ppermute | solution.py:70
  121.8 1.0 collective-permute-done.23
  122.8 0.7 add.114
  123.5 0.8 collective-permute-start.24
  124.3 2.8 %collective-permute-done.24 = f32[2,4,16]{2,1,0:T(4,128)S(1)} collective-permute-done((f32[2,4,16]{2,1,0:T(4,128)S(1)}, f32[2,4,16]{2,1,0:T(4,128)S(1)}, u32[]{:S(2)}, u32[]{:S(2)}) %collective-permute-start.24) | collective-permute-done | bytes 544 | tf_op jit(solution)/shard_map/ppermute | solution.py:70
  127.1 1.5 collective-permute-start.25
  128.5 3.4 %collective-permute-done.25 = f32[2,4,16]{2,1,0:T(4,128)S(1)} collective-permute-done((f32[2,4,16]{2,1,0:T(4,128)S(1)}, f32[2,4,16]{2,1,0:T(4,128)S(1)}, u32[]{:S(2)}, u32[]{:S(2)}) %collective-permute-start.25) | collective-permute-done | bytes 544 | tf_op jit(solution)/shard_map/ppermute | solution.py:70
  131.9 1.5 collective-permute-start.26
  133.4 2.1 %collective-permute-done.26 = f32[2,4,16]{2,1,0:T(4,128)S(1)} collective-permute-done((f32[2,4,16]{2,1,0:T(4,128)S(1)}, f32[2,4,16]{2,1,0:T(4,128)S(1)}, u32[]{:S(2)}, u32[]{:S(2)}) %collective-permute-start.26) | collective-permute-done | bytes 544 | tf_op jit(solution)/shard_map/ppermute | solution.py:70
  135.5 1.2 collective-permute-start.27
  136.7 3.6 %collective-permute-done.27 = f32[2,4,16]{2,1,0:T(4,128)S(1)} collective-permute-done((f32[2,4,16]{2,1,0:T(4,128)S(1)}, f32[2,4,16]{2,1,0:T(4,128)S(1)}, u32[]{:S(2)}, u32[]{:S(2)}) %collective-permute-start.27) | collective-permute-done | bytes 544 | tf_op jit(solution)/shard_map/ppermute | solution.py:70
  140.3 2.5 %collective-permute-start.28 = (f32[2,4,16]{2,1,0:T(4,128)S(1)}, f32[2,4,16]{2,1,0:T(4,128)S(1)}, u32[]{:S(2)}, u32[]{:S(2)}) collective-permute-start(f32[2,4,16]{2,1,0:T(4,128)S(1)} %add.118), channel_id=1, source_target_pairs={{0,4},{1,5},{2,6},{3,7},{4,0},{5,1},{6,2},{7,3},{8,12},{9,13},{10,... | collective-permute-start | bytes 1544 | tf_op jit(solution)/shard_map/ppermute | solution.py:70
  142.8 1.6 %collective-permute-done.28 = f32[2,4,16]{2,1,0:T(4,128)S(1)} collective-permute-done((f32[2,4,16]{2,1,0:T(4,128)S(1)}, f32[2,4,16]{2,1,0:T(4,128)S(1)}, u32[]{:S(2)}, u32[]{:S(2)}) %collective-permute-start.28) | collective-permute-done | bytes 544 | tf_op jit(solution)/shard_map/ppermute | solution.py:70
  144.4 3.9 %collective-permute-start.29 = (f32[2,4,16]{2,1,0:T(4,128)S(1)}, f32[2,4,16]{2,1,0:T(4,128)S(1)}, u32[]{:S(2)}, u32[]{:S(2)}) collective-permute-start(f32[2,4,16]{2,1,0:T(4,128)S(1)} %add.119), channel_id=1, source_target_pairs={{0,12},{1,13},{2,14},{3,15},{4,8},{5,9},{6,10},{7,11},{8,4},{9,5},... | collective-permute-start | bytes 1544 | tf_op jit(solution)/shard_map/ppermute | solution.py:70
  148.3 1.6 %collective-permute-done.29 = f32[2,4,16]{2,1,0:T(4,128)S(1)} collective-permute-done((f32[2,4,16]{2,1,0:T(4,128)S(1)}, f32[2,4,16]{2,1,0:T(4,128)S(1)}, u32[]{:S(2)}, u32[]{:S(2)}) %collective-permute-start.29) | collective-permute-done | bytes 544 | tf_op jit(solution)/shard_map/ppermute | solution.py:70
  149.9 0.6 add.120
  (52 shorter events, 0.3 us)
Async XLA Ops:
  0.0 76.0 %copy-start = (bf16[2,1024,128]{2,1,0:T(8,128)(2,1)S(1)}, bf16[2,1024,128]{2,1,0:T(8,128)(2,1)}, u32[]{:S(2)}) copy-start(bf16[2,1024,128]{2,1,0:T(8,128)(2,1)} %refs_0_.3) | copy-start | bytes 1572868
  0.0 15.4 %collective-permute-start.11 = (bf16[2,1024,128]{2,1,0:T(8,128)(2,1)}, bf16[2,1024,128]{2,1,0:T(8,128)(2,1)S(1)}, u32[]{:S(2)}, u32[]{:S(2)}) collective-permute-start(bf16[2,1024,128]{2,1,0:T(8,128)(2,1)} %refs_0_.3), channel_id=1, source_target_pairs={{0,2},{1,3},{2,0},{3,1},{4,6},{5,7},{6,4},{7,5},{8,10},{9,11},{10,... | collective-permute-start | bytes 1572872 | tf_op jit(solution)/shard_map/ppermute | solution.py:70
  3.1 20.2 %collective-permute-start.8 = (bf16[2,1024,128]{2,1,0:T(8,128)(2,1)}, bf16[2,1024,128]{2,1,0:T(8,128)(2,1)S(1)}, u32[]{:S(2)}, u32[]{:S(2)}) collective-permute-start(bf16[2,1024,128]{2,1,0:T(8,128)(2,1)} %refs_0_.3), channel_id=1, source_target_pairs={{0,4},{1,5},{2,6},{3,7},{4,8},{5,9},{6,10},{7,11},{8,12},{9,13},{1... | collective-permute-start | bytes 1572872 | tf_op jit(solution)/shard_map/ppermute | solution.py:70
  5.0 18.3 %collective-permute-start.9 = (bf16[2,1024,128]{2,1,0:T(8,128)(2,1)}, bf16[2,1024,128]{2,1,0:T(8,128)(2,1)S(1)}, u32[]{:S(2)}, u32[]{:S(2)}) collective-permute-start(bf16[2,1024,128]{2,1,0:T(8,128)(2,1)} %refs_0_.3), channel_id=1, source_target_pairs={{0,12},{1,13},{2,14},{3,15},{4,0},{5,1},{6,2},{7,3},{8,4},{9,5},{1... | collective-permute-start | bytes 1572872 | tf_op jit(solution)/shard_map/ppermute | solution.py:70
  7.2 20.6 %collective-permute-start = (bf16[2,1024,128]{2,1,0:T(8,128)(2,1)}, bf16[2,1024,128]{2,1,0:T(8,128)(2,1)}, u32[]{:S(2)}, u32[]{:S(2)}) collective-permute-start(bf16[2,1024,128]{2,1,0:T(8,128)(2,1)} %refs_0_.3), channel_id=1, source_target_pairs={{0,32},{1,0},{2,80},{3,112},{4,16},{5,48},{6,64},{7,96},{8,33},{9,... | collective-permute-start | bytes 1572872 | tf_op jit(solution)/shard_map/ppermute | solution.py:70
  15.4 17.6 %collective-permute-start.12 = (bf16[2,1024,128]{2,1,0:T(8,128)(2,1)S(1)}, bf16[2,1024,128]{2,1,0:T(8,128)(2,1)S(1)}, u32[]{:S(2)}, u32[]{:S(2)}) collective-permute-start(bf16[2,1024,128]{2,1,0:T(8,128)(2,1)S(1)} %collective-permute-done.11.refs_4_), channel_id=1, source_target_pairs={{0,4},{1,5},{2,6},{3,7},{4,8},{5,9},{6,10},{7,11},{8,12},{9,13},{1... | collective-permute-start | bytes 1572872 | tf_op jit(solution)/shard_map/ppermute | solution.py:70
  17.5 22.0 %collective-permute-start.13 = (bf16[2,1024,128]{2,1,0:T(8,128)(2,1)S(1)}, bf16[2,1024,128]{2,1,0:T(8,128)(2,1)S(1)}, u32[]{:S(2)}, u32[]{:S(2)}) collective-permute-start(bf16[2,1024,128]{2,1,0:T(8,128)(2,1)S(1)} %collective-permute-done.11.refs_4_), channel_id=1, source_target_pairs={{0,12},{1,13},{2,14},{3,15},{4,0},{5,1},{6,2},{7,3},{8,4},{9,5},{1... | collective-permute-start | bytes 1572872 | tf_op jit(solution)/shard_map/ppermute | solution.py:70
  23.3 20.9 %collective-permute-start.15 = (bf16[2,1024,128]{2,1,0:T(8,128)(2,1)}, bf16[2,1024,128]{2,1,0:T(8,128)(2,1)S(1)}, u32[]{:S(2)}, u32[]{:S(2)}) collective-permute-start(bf16[2,1024,128]{2,1,0:T(8,128)(2,1)} %refs_0_.3), channel_id=1, source_target_pairs={{0,1},{1,0},{2,3},{3,2},{4,5},{5,4},{6,7},{7,6},{8,9},{9,8},{10,11... | collective-permute-start | bytes 1572872 | tf_op jit(solution)/shard_map/ppermute | solution.py:70
  23.4 21.6 %collective-permute-start.10 = (bf16[2,1024,128]{2,1,0:T(8,128)(2,1)S(1)}, bf16[2,1024,128]{2,1,0:T(8,128)(2,1)S(1)}, u32[]{:S(2)}, u32[]{:S(2)}) collective-permute-start(bf16[2,1024,128]{2,1,0:T(8,128)(2,1)S(1)} %broadcast_select_fusion.1), channel_id=1, source_target_pairs={{0,4},{1,13},{2,6},{3,15},{4,8},{5,1},{6,10},{7,3},{8,12},{9,5},{1... | collective-permute-start | bytes 1572872 | tf_op jit(solution)/shard_map/ppermute | solution.py:70
  27.8 20.5 %collective-permute-start.19 = (bf16[2,1024,128]{2,1,0:T(8,128)(2,1)S(1)}, bf16[2,1024,128]{2,1,0:T(8,128)(2,1)S(1)}, u32[]{:S(2)}, u32[]{:S(2)}) collective-permute-start(bf16[2,1024,128]{2,1,0:T(8,128)(2,1)S(1)} %collective-permute-done.11.refs_4_), channel_id=1, source_target_pairs={{0,1},{1,0},{2,3},{3,2},{4,5},{5,4},{6,7},{7,6},{8,9},{9,8},{10,11... | collective-permute-start | bytes 1572872 | tf_op jit(solution)/shard_map/ppermute | solution.py:70
  33.0 21.7 %collective-permute-start.16 = (bf16[2,1024,128]{2,1,0:T(8,128)(2,1)S(1)}, bf16[2,1024,128]{2,1,0:T(8,128)(2,1)S(1)}, u32[]{:S(2)}, u32[]{:S(2)}) collective-permute-start(bf16[2,1024,128]{2,1,0:T(8,128)(2,1)S(1)} %collective-permute-done.8.refs_1_), channel_id=1, source_target_pairs={{0,1},{1,0},{2,3},{3,2},{4,5},{5,4},{6,7},{7,6},{8,9},{9,8},{10,11... | collective-permute-start | bytes 1572872 | tf_op jit(solution)/shard_map/ppermute | solution.py:70
  39.4 15.3 %collective-permute-start.4 = (bf16[2,1024,128]{2,1,0:T(8,128)(2,1)}, bf16[2,1024,128]{2,1,0:T(8,128)(2,1)}, u32[]{:S(2)}, u32[]{:S(2)}) collective-permute-start(bf16[2,1024,128]{2,1,0:T(8,128)(2,1)} %collective-permute-done.refs_0_), channel_id=1, source_target_pairs={{0,64},{1,65},{2,66},{3,67},{4,68},{5,69},{6,70},{7,71},{8,72},{9,... | collective-permute-start | bytes 1572872 | tf_op jit(solution)/shard_map/ppermute | solution.py:70
  44.2 0.8 copy-start.1
  45.0 18.9 %collective-permute-start.1 = (bf16[2,1024,128]{2,1,0:T(8,128)(2,1)}, bf16[2,1024,128]{2,1,0:T(8,128)(2,1)}, u32[]{:S(2)}, u32[]{:S(2)}) collective-permute-start(bf16[2,1024,128]{2,1,0:T(8,128)(2,1)} %collective-permute-done.refs_0_), channel_id=1, source_target_pairs={{0,16},{1,17},{2,18},{3,19},{4,20},{5,21},{6,22},{7,23},{8,24},{9,... | collective-permute-start | bytes 1572872 | tf_op jit(solution)/shard_map/ppermute | solution.py:70
  45.0 9.7 %copy-start.3 = (bf16[2,1024,128]{2,1,0:T(8,128)(2,1)}, bf16[2,1024,128]{2,1,0:T(8,128)(2,1)S(1)}, u32[]{:S(2)}) copy-start(bf16[2,1024,128]{2,1,0:T(8,128)(2,1)S(1)} %collective-permute-done.10.refs_3_) | copy-start | bytes 1572868
  45.0 18.9 %collective-permute-start.2 = (bf16[2,1024,128]{2,1,0:T(8,128)(2,1)}, bf16[2,1024,128]{2,1,0:T(8,128)(2,1)}, u32[]{:S(2)}, u32[]{:S(2)}) collective-permute-start(bf16[2,1024,128]{2,1,0:T(8,128)(2,1)} %collective-permute-done.refs_0_), channel_id=1, source_target_pairs={{0,48},{1,49},{2,50},{3,51},{4,52},{5,53},{6,54},{7,55},{8,56},{9,... | collective-permute-start | bytes 1572872 | tf_op jit(solution)/shard_map/ppermute | solution.py:70
  48.3 10.5 %copy-start.7 = (bf16[2,1024,128]{2,1,0:T(8,128)(2,1)}, bf16[2,1024,128]{2,1,0:T(8,128)(2,1)S(1)}, u32[]{:S(2)}) copy-start(bf16[2,1024,128]{2,1,0:T(8,128)(2,1)S(1)} %collective-permute-done.19.refs_12_) | copy-start | bytes 1572868
  48.3 16.1 %collective-permute-start.14 = (bf16[2,1024,128]{2,1,0:T(8,128)(2,1)}, bf16[2,1024,128]{2,1,0:T(8,128)(2,1)}, u32[]{:S(2)}, u32[]{:S(2)}) collective-permute-start(bf16[2,1024,128]{2,1,0:T(8,128)(2,1)} %broadcast_select_fusion), channel_id=1, source_target_pairs={{0,4},{1,13},{2,6},{3,15},{4,8},{5,1},{6,10},{7,3},{8,12},{9,5},{1... | collective-permute-start | bytes 1572872 | tf_op jit(solution)/shard_map/ppermute | solution.py:70
  54.7 15.7 %collective-permute-start.5 = (bf16[2,1024,128]{2,1,0:T(8,128)(2,1)}, bf16[2,1024,128]{2,1,0:T(8,128)(2,1)}, u32[]{:S(2)}, u32[]{:S(2)}) collective-permute-start(bf16[2,1024,128]{2,1,0:T(8,128)(2,1)} %collective-permute-done.4.refs_4_), channel_id=1, source_target_pairs={{0,16},{1,17},{2,18},{3,19},{4,20},{5,21},{6,22},{7,23},{8,24},{9,... | collective-permute-start | bytes 1572872 | tf_op jit(solution)/shard_map/ppermute | solution.py:70
  54.7 0.8 copy-start.5
  55.5 15.0 %collective-permute-start.6 = (bf16[2,1024,128]{2,1,0:T(8,128)(2,1)}, bf16[2,1024,128]{2,1,0:T(8,128)(2,1)}, u32[]{:S(2)}, u32[]{:S(2)}) collective-permute-start(bf16[2,1024,128]{2,1,0:T(8,128)(2,1)} %collective-permute-done.4.refs_4_), channel_id=1, source_target_pairs={{0,48},{1,49},{2,50},{3,51},{4,52},{5,53},{6,54},{7,55},{8,56},{9,... | collective-permute-start | bytes 1572872 | tf_op jit(solution)/shard_map/ppermute | solution.py:70
  63.9 9.3 %collective-permute-start.17 = (bf16[2,1024,128]{2,1,0:T(8,128)(2,1)S(1)}, bf16[2,1024,128]{2,1,0:T(8,128)(2,1)S(1)}, u32[]{:S(2)}, u32[]{:S(2)}) collective-permute-start(bf16[2,1024,128]{2,1,0:T(8,128)(2,1)S(1)} %collective-permute-done.9.refs_2_), channel_id=1, source_target_pairs={{0,1},{1,0},{2,3},{3,2},{4,5},{5,4},{6,7},{7,6},{8,9},{9,8},{10,11... | collective-permute-start | bytes 1572872 | tf_op jit(solution)/shard_map/ppermute | solution.py:70
  63.9 10.4 %collective-permute-start.20 = (bf16[2,1024,128]{2,1,0:T(8,128)(2,1)S(1)}, bf16[2,1024,128]{2,1,0:T(8,128)(2,1)S(1)}, u32[]{:S(2)}, u32[]{:S(2)}) collective-permute-start(bf16[2,1024,128]{2,1,0:T(8,128)(2,1)S(1)} %collective-permute-done.12.refs_5_), channel_id=1, source_target_pairs={{0,1},{1,0},{2,3},{3,2},{4,5},{5,4},{6,7},{7,6},{8,9},{9,8},{10,11... | collective-permute-start | bytes 1572872 | tf_op jit(solution)/shard_map/ppermute | solution.py:70
  64.4 9.9 %collective-permute-start.21 = (bf16[2,1024,128]{2,1,0:T(8,128)(2,1)S(1)}, bf16[2,1024,128]{2,1,0:T(8,128)(2,1)S(1)}, u32[]{:S(2)}, u32[]{:S(2)}) collective-permute-start(bf16[2,1024,128]{2,1,0:T(8,128)(2,1)S(1)} %collective-permute-done.13.refs_6_), channel_id=1, source_target_pairs={{0,1},{1,0},{2,3},{3,2},{4,5},{5,4},{6,7},{7,6},{8,9},{9,8},{10,11... | collective-permute-start | bytes 1572872 | tf_op jit(solution)/shard_map/ppermute | solution.py:70
  70.5 2.8 %collective-permute-start.18 = (bf16[2,1024,128]{2,1,0:T(8,128)(2,1)}, bf16[2,1024,128]{2,1,0:T(8,128)(2,1)S(1)}, u32[]{:S(2)}, u32[]{:S(2)}) collective-permute-start(bf16[2,1024,128]{2,1,0:T(8,128)(2,1)} %copy-done.3), channel_id=1, source_target_pairs={{0,1},{1,0},{2,3},{3,2},{4,5},{5,4},{6,7},{7,6},{8,9},{9,8},{10,11... | collective-permute-start | bytes 1572872 | tf_op jit(solution)/shard_map/ppermute | solution.py:70
  70.5 3.8 %collective-permute-start.22 = (bf16[2,1024,128]{2,1,0:T(8,128)(2,1)}, bf16[2,1024,128]{2,1,0:T(8,128)(2,1)S(1)}, u32[]{:S(2)}, u32[]{:S(2)}) collective-permute-start(bf16[2,1024,128]{2,1,0:T(8,128)(2,1)} %collective-permute-done.14.refs_7_), channel_id=1, source_target_pairs={{0,1},{1,0},{2,3},{3,2},{4,5},{5,4},{6,7},{7,6},{8,9},{9,8},{10,11... | collective-permute-start | bytes 1572872 | tf_op jit(solution)/shard_map/ppermute | solution.py:70
  73.2 37.5 %collective-permute-start.3 = (bf16[2,1024,128]{2,1,0:T(8,128)(2,1)S(1)}, bf16[2,1024,128]{2,1,0:T(8,128)(2,1)}, u32[]{:S(2)}, u32[]{:S(2)}) collective-permute-start(bf16[2,1024,128]{2,1,0:T(8,128)(2,1)S(1)} %broadcast_select_fusion.3), channel_id=1, source_target_pairs={{0,16},{1,49},{2,18},{3,51},{4,20},{5,53},{6,22},{7,55},{8,24},{9,... | collective-permute-start | bytes 1572872 | tf_op jit(solution)/shard_map/ppermute | solution.py:70
  73.3 1.0 copy-start.10
  73.3 37.4 %collective-permute-start.7 = (bf16[2,1024,128]{2,1,0:T(8,128)(2,1)S(1)}, bf16[2,1024,128]{2,1,0:T(8,128)(2,1)}, u32[]{:S(2)}, u32[]{:S(2)}) collective-permute-start(bf16[2,1024,128]{2,1,0:T(8,128)(2,1)S(1)} %broadcast_select_fusion.2), channel_id=1, source_target_pairs={{0,16},{1,49},{2,18},{3,51},{4,20},{5,53},{6,22},{7,55},{8,24},{9,... | collective-permute-start | bytes 1572872 | tf_op jit(solution)/shard_map/ppermute | solution.py:70
  74.2 0.8 copy-start.8
  74.3 1.0 copy-start.9
  75.2 0.8 copy-start.11
  76.0 1.0 copy-start.2
  77.1 1.0 copy-start.4
  78.1 1.0 copy-start.6
  119.7 3.1 %collective-permute-start.23 = (f32[2,4,16]{2,1,0:T(4,128)}, f32[2,4,16]{2,1,0:T(4,128)S(1)}, u32[]{:S(2)}, u32[]{:S(2)}) collective-permute-start(f32[2,4,16]{2,1,0:T(4,128)} %shard_map.75), channel_id=1, source_target_pairs={{0,1},{1,0},{2,3},{3,2},{4,5},{5,4},{6,7},{7,6},{8,9},{9,8},{10,11... | collective-permute-start | bytes 1544 | tf_op jit(solution)/shard_map/ppermute | solution.py:70
  123.5 3.6 %collective-permute-start.24 = (f32[2,4,16]{2,1,0:T(4,128)S(1)}, f32[2,4,16]{2,1,0:T(4,128)S(1)}, u32[]{:S(2)}, u32[]{:S(2)}) collective-permute-start(f32[2,4,16]{2,1,0:T(4,128)S(1)} %add.114), channel_id=1, source_target_pairs={{0,64},{1,65},{2,66},{3,67},{4,68},{5,69},{6,70},{7,71},{8,72},{9,... | collective-permute-start | bytes 1544 | tf_op jit(solution)/shard_map/ppermute | solution.py:70
  127.1 4.8 %collective-permute-start.25 = (f32[2,4,16]{2,1,0:T(4,128)S(1)}, f32[2,4,16]{2,1,0:T(4,128)S(1)}, u32[]{:S(2)}, u32[]{:S(2)}) collective-permute-start(f32[2,4,16]{2,1,0:T(4,128)S(1)} %add.115), channel_id=1, source_target_pairs={{0,66},{1,67},{2,64},{3,65},{4,70},{5,71},{6,68},{7,69},{8,74},{9,... | collective-permute-start | bytes 1544 | tf_op jit(solution)/shard_map/ppermute | solution.py:70
  131.9 3.6 %collective-permute-start.26 = (f32[2,4,16]{2,1,0:T(4,128)S(1)}, f32[2,4,16]{2,1,0:T(4,128)S(1)}, u32[]{:S(2)}, u32[]{:S(2)}) collective-permute-start(f32[2,4,16]{2,1,0:T(4,128)S(1)} %add.116), channel_id=1, source_target_pairs={{0,16},{1,17},{2,18},{3,19},{4,20},{5,21},{6,22},{7,23},{8,24},{9,... | collective-permute-start | bytes 1544 | tf_op jit(solution)/shard_map/ppermute | solution.py:70
  135.5 4.8 %collective-permute-start.27 = (f32[2,4,16]{2,1,0:T(4,128)S(1)}, f32[2,4,16]{2,1,0:T(4,128)S(1)}, u32[]{:S(2)}, u32[]{:S(2)}) collective-permute-start(f32[2,4,16]{2,1,0:T(4,128)S(1)} %add.117), channel_id=1, source_target_pairs={{0,48},{1,49},{2,50},{3,51},{4,52},{5,53},{6,54},{7,55},{8,56},{9,... | collective-permute-start | bytes 1544 | tf_op jit(solution)/shard_map/ppermute | solution.py:70
  140.3 4.0 %collective-permute-start.28 = (f32[2,4,16]{2,1,0:T(4,128)S(1)}, f32[2,4,16]{2,1,0:T(4,128)S(1)}, u32[]{:S(2)}, u32[]{:S(2)}) collective-permute-start(f32[2,4,16]{2,1,0:T(4,128)S(1)} %add.118), channel_id=1, source_target_pairs={{0,4},{1,5},{2,6},{3,7},{4,0},{5,1},{6,2},{7,3},{8,12},{9,13},{10,... | collective-permute-start | bytes 1544 | tf_op jit(solution)/shard_map/ppermute | solution.py:70
  144.4 5.5 %collective-permute-start.29 = (f32[2,4,16]{2,1,0:T(4,128)S(1)}, f32[2,4,16]{2,1,0:T(4,128)S(1)}, u32[]{:S(2)}, u32[]{:S(2)}) collective-permute-start(f32[2,4,16]{2,1,0:T(4,128)S(1)} %add.119), channel_id=1, source_target_pairs={{0,12},{1,13},{2,14},{3,15},{4,8},{5,9},{6,10},{7,11},{8,4},{9,5},... | collective-permute-start | bytes 1544 | tf_op jit(solution)/shard_map/ppermute | solution.py:70

commit v2 on v0

v2 whole, which is shorter than its diff:
```python
import functools
import itertools

import jax
import jax.numpy as jnp
from jax import lax
from jax.experimental import pallas as pl
from jax.experimental.pallas import tpu as pltpu
from jax.sharding import Mesh
from jax.sharding import PartitionSpec as P

AXES = ("x_lo", "y", "z", "x_hi", "core")
ROW = ("x_lo", "y")
COL = ("z", "x_hi", "core")
STEP = 128
SCALE = 256 ** (-0.5)

MATCH = (
    (2, 0, 5, 7, 1, 3, 4, 6),
    (2, 3, 5, 4, 1, 0, 7, 6),
    (7, 4, 3, 1, 6, 5, 0, 2),
    (6, 7, 0, 2, 4, 5, 3, 1),
    (2, 0, 5, 4, 1, 3, 7, 6),
    (2, 0, 5, 4, 3, 1, 6, 7),
    (6, 4, 2, 1, 7, 5, 0, 3),
    (4, 6, 2, 0, 5, 7, 3, 1),
    (6, 4, 3, 1, 5, 7, 0, 2),
    (6, 7, 1, 0, 4, 5, 3, 2),
    (2, 0, 5, 6, 1, 3, 7, 4),
    (1, 3, 5, 4, 2, 0, 6, 7),
    (7, 6, 3, 1, 5, 4, 0, 2),
    (6, 7, 3, 1, 4, 5, 2, 0),
    (3, 0, 5, 7, 1, 2, 4, 6),
    (1, 3, 7, 5, 0, 2, 4, 6),
)


def pairs_of(move):
    found = []
    for x_lo, y, z, x_hi, core in itertools.product(range(2), range(4), range(4), range(2), range(2)):
        x, ny, nz, ncore = move(2 * x_hi + x_lo, y, z, core)
        x, ny, nz = x % 4, ny % 4, nz % 4
        source = (((x_lo * 4 + y) * 4 + z) * 2 + x_hi) * 2 + core
        found.append((source, (((x % 2 * 4 + ny) * 4 + nz) * 2 + x // 2) * 2 + ncore))
    return found


Z_ON = pairs_of(lambda x, y, z, c: (x, y, z + 1 - 2 * c, c))
Z_BACK = pairs_of(lambda x, y, z, c: (x, y, z - 1 + 2 * c, c))
Y_ON = pairs_of(lambda x, y, z, c: (x, y + 1 - 2 * c, z, c))
Y_FAR = pairs_of(lambda x, y, z, c: (x, y + 2, z, c))
Y_BACK = pairs_of(lambda x, y, z, c: (x, y - 1 + 2 * c, z, c))
X_FAR = pairs_of(lambda x, y, z, c: (x + 2, y, z, c))
X_NEAR = pairs_of(lambda x, y, z, c: (x ^ 1, y, z, c))
CORE = pairs_of(lambda x, y, z, c: (x, y, z, 1 - c))
TURN = [(c // 2 * 16 + c % 2 * 8 + j, MATCH[c][j] * 16 + c) for c in range(16) for j in range(8)]
ROUNDS = (
    CORE,
    X_NEAR,
    pairs_of(lambda x, y, z, c: (x + (1 if x % 2 else -1), y, z, c)),
    pairs_of(lambda x, y, z, c: (x, y ^ 1, z, c)),
    pairs_of(lambda x, y, z, c: (x, y + (1 if y % 2 else -1), z, c)),
    pairs_of(lambda x, y, z, c: (x, y, z ^ 1, c)),
    pairs_of(lambda x, y, z, c: (x, y, z + (1 if z % 2 else -1), c)),
)


def send(block, pairs):
    return lax.ppermute(block, AXES, pairs)


def after(value, *others):
    return lax.optimization_barrier((value, *others))[0]


def meet(*values):
    return lax.optimization_barrier(values)


def weights(energy_grid, band_index, energy_index):
    points = lax.broadcasted_iota(jnp.int32, (1, energy_grid.shape[0]), 1)
    band_energy = jnp.sum(
        jnp.where(band_index[:, None] == points, energy_grid[None, :], 0.0), axis=-1
    )
    eval_energy = jnp.sum(
        jnp.where(energy_index[:, :, None] == points[None], energy_grid[None, None, :], 0.0),
        axis=-1,
    )
    offset = eval_energy[:, None, :] - band_energy[None, :, None]
    denom = offset * offset + 0.25
    w = jnp.stack([offset / denom, -0.5 / denom])
    return w.reshape(2, -1, w.shape[-1])


VMEM = pl.BlockSpec(memory_space=pltpu.VMEM)


ANY = pl.BlockSpec(memory_space=pl.ANY)
HBM = pl.BlockSpec(memory_space=pltpu.HBM)


def keep_body(w_ref, out):
    out[...] = w_ref[...]


def keep(w):
    return pl.pallas_call(
        keep_body,
        out_shape=jax.ShapeDtypeStruct(w.shape, w.dtype),
        in_specs=[VMEM],
        out_specs=VMEM,
    )(w)


def product_body(first, pack, tags, *refs):
    refs = list(refs)
    blocks = [refs.pop(0) for _ in range(1 if "packed" in tags[-1] else len(tags))]
    if len(blocks) < len(tags):
        blocks = [blocks[0].at[i] for i in range(len(tags))]
    blocks = [block for block, tag in zip(blocks, tags, strict=True) if tag[2] != "skip"]
    tags = [tag for tag in tags if tag[2] != "skip"]
    count = len(tags)
    w_hbm = refs.pop(0)
    if not first:
        refs.pop(0)
    z_ref = refs.pop(0)
    out = refs.pop(0) if pack else None
    block_buf, w_buf, sems = refs
    z = lax.axis_index("z")
    copies = []
    for i, (past, back, other) in enumerate(tags):
        core, x_hi = lax.axis_index("core"), lax.axis_index("x_hi")
        core = 1 - core if other else core
        x_hi = 1 - x_hi if past else x_hi
        layer = (z + 4 - (1 - 2 * core) * back) & 3
        at = pl.multiple_of((layer * 4 + x_hi * 2 + core) * STEP, STEP)
        copies.append(pltpu.make_async_copy(blocks[i], block_buf.at[i], sems.at[0, i]))
        copies.append(pltpu.make_async_copy(w_hbm.at[:, pl.ds(at, STEP), :], w_buf.at[i], sems.at[1, i]))
    for copy in copies:
        copy.start()
    for some in (range(1), range(1, count)):
        for copy in copies[2 * some.start : 2 * some.stop]:
            copy.wait()
        if pack and some.start == 1:
            saved = pltpu.make_async_copy(block_buf, out, sems.at[2, 0])
            saved.start()
        w_re, w_im = [], []
        for i in some:
            x, y = w_buf[i, 0], w_buf[i, 1]
            w_re += [x, y]
            w_im += [y, -x]
        w_re, w_im = jnp.concatenate(w_re, axis=0), jnp.concatenate(w_im, axis=0)
        for m in range(2):
            at = pl.ds(m * 512, 512)
            lhs = jnp.concatenate([block_buf[i, part, at, :] for i in some for part in (0, 1)], axis=1)
            for part, w in ((0, w_re), (1, w_im)):
                value = jnp.dot(lhs, w, preferred_element_type=jnp.float32)
                if first and some.start == 0:
                    z_ref[part, at, :] = value
                else:
                    z_ref[part, at, :] += value
    if pack:
        saved.wait()


def product(tags, blocks, screened, z=None, pack=False):
    count = len(tags)
    args = [*blocks, screened]
    specs = [HBM] * len(args)
    shapes, outs = [jax.ShapeDtypeStruct((2, 1024, 1024), jnp.float32)], [VMEM]
    alias = {}
    if z is not None:
        args.append(z)
        specs.append(VMEM)
        alias = {len(args) - 1: 0}
    if pack:
        shapes.append(jax.ShapeDtypeStruct((count, 2, 1024, STEP), jnp.bfloat16))
        outs.append(HBM)
    return pl.pallas_call(
        functools.partial(product_body, z is None, pack, tags),
        out_shape=shapes,
        in_specs=specs,
        out_specs=outs,
        scratch_shapes=[
            pltpu.VMEM((count, 2, 1024, STEP), jnp.bfloat16),
            pltpu.VMEM((count, 2, STEP, 1024), jnp.bfloat16),
            pltpu.SemaphoreType.DMA((3, count)),
        ],
        input_output_aliases=alias,
        compiler_params=pltpu.CompilerParams(vmem_limit_bytes=40 << 20),
        cost_estimate=pl.CostEstimate(flops=1, transcendentals=0, bytes_accessed=1),
    )(*args)


def form_body(tags, *refs):
    count = len(tags)
    blocks, z_ref, w_ref, out = refs[:count], refs[count], refs[count + 1], refs[-1]
    group = (lax.axis_index("z") * 2 + lax.axis_index("x_hi")) * 2 + lax.axis_index("core")
    code = jnp.int32(0)
    for c in range(16):
        code = jnp.where(group == c, CODES[c], code)
    places = []
    for beside, back in tags:
        x_lo = lax.axis_index("x_lo")
        x_lo = 1 - x_lo if beside else x_lo
        way = 1 - 2 * lax.axis_index("core")
        source = x_lo * 4 + ((lax.axis_index("y") + 4 - way * back) & 3)
        places.append(pl.ds(pl.multiple_of(((code >> (3 * source)) & 7) * STEP, STEP), STEP))

    for n in range(4):
        o_re = jnp.zeros((1, 16), jnp.float32)
        o_im = jnp.zeros((1, 16), jnp.float32)
        for half in range(2):
            rows = pl.ds(n * 256 + half * STEP, STEP)
            s_re = jnp.zeros((STEP, STEP), jnp.float32)
            s_im = jnp.zeros((STEP, STEP), jnp.float32)
            for block, at in zip(blocks, places, strict=True):
                z_re, z_im = z_ref[0, rows, at], z_ref[1, rows, at]
                re, im = block[0, rows, :].astype(jnp.float32), block[1, rows, :].astype(jnp.float32)
                s_re += z_re * re - z_im * im
                s_im += z_re * im + z_im * re
            s_re = jnp.sum(s_re, axis=1, keepdims=True)
            s_im = jnp.sum(s_im, axis=1, keepdims=True)
            w_re, w_im = w_ref[0, rows, :], w_ref[1, rows, :]
            o_re += jnp.sum(w_re * s_re - w_im * s_im, axis=0, keepdims=True)
            o_im += jnp.sum(w_re * s_im + w_im * s_re, axis=0, keepdims=True)
        for part, o in ((0, o_re), (1, o_im)):
            o = o * SCALE
            if len(refs) > count + 3:
                o += refs[count + 2][part, n : n + 1, :]
            out[part, n : n + 1, :] = o


CODES = [sum(row.index(r) << (3 * r) for r in range(8)) for row in MATCH]


def form(tags, blocks, z, w, total=None):
    args = [*blocks, z, w] + ([] if total is None else [total])
    return pl.pallas_call(
        functools.partial(form_body, tags),
        out_shape=jax.ShapeDtypeStruct((2, 4, 16), jnp.float32),
        in_specs=[VMEM] * len(args),
        out_specs=VMEM,
        compiler_params=pltpu.CompilerParams(vmem_limit_bytes=8 << 20),
        cost_estimate=pl.CostEstimate(flops=1, transcendentals=0, bytes_accessed=1),
    )(*args)


def local(screened, elements, energy_grid, band_index, energy_index):
    w = keep(weights(energy_grid, band_index, energy_index))

    t0 = send(elements, TURN)
    p0 = send(elements, X_FAR)
    n1, n3 = send(elements, Z_ON), send(elements, Z_BACK)
    m0 = send(elements, CORE)
    n1, n3, w = meet(n1, n3, w)
    m1, m3, q0 = send(n1, CORE), send(n3, CORE), send(p0, CORE)
    t0, p0, n1, n3, m0, m1, m3, q0 = meet(t0, p0, n1, n3, m0, m1, m3, q0)

    t1, t3, t2 = send(t0, Y_ON), send(t0, Y_BACK), send(t0, Y_FAR)
    u0 = send(t0, X_NEAR)
    n2 = send(n1, Z_ON)
    z, = product(((0, 0, False), (0, 1, False), (0, 3, False), (1, 0, False)), [elements, n1, n3, p0], screened)
    p2 = send(n2, X_FAR)
    late = after(p0, n2)
    p1, p3 = send(late, Z_ON), send(late, Z_BACK)
    z, = product(((0, 0, True), (0, 1, True), (0, 3, True), (1, 0, True)), [m0, m1, m3, q0], screened, z)
    t1, t3, t2, u0, n2, p2, p1, p3, z = meet(t1, t3, t2, u0, n2, p2, p1, p3, z)

    u1, u3, u2 = send(u0, Y_ON), send(u0, Y_BACK), send(t2, X_NEAR)
    m2, q2, q1, q3 = [send(block, CORE) for block in (n2, p2, p1, p3)]
    z, = product(((0, 2, False), (1, 1, False), (1, 2, False), (1, 3, False)), [n2, p1, p2, p3], screened, z)
    z, = product(((0, 2, True), (1, 1, True), (1, 2, True), (1, 3, True)), [m2, q1, q2, q3], screened, z)
    tags = ((0, 0), (0, 1), (0, 2), (0, 3), (1, 0), (1, 1), (1, 3), (1, 2))
    out = form(tags, [t0, t1, t2, t3, u0, u1, u3, u2], z, w)
    for pairs in ROUNDS:
        out = out + send(out, pairs)
    return out


def solution(mesh):
    split = Mesh(mesh.devices.reshape(2, 4, 4, 2, 2), AXES)
    in_specs = (P(None, ROW, COL), P(None, None, ROW + COL), P(), P(), P())
    return jax.shard_map(local, mesh=split, in_specs=in_specs, out_specs=P(), check_vma=False)
```

time: 312 us -> 115 us (0.37)
  waiting for transfers between devices: 185 us -> 30.6 us
  blocking collectives: 64.6 us -> 0 us
  starting transfers between devices: 0.04 us -> 50.7 us
  Pallas kernels: 0 us -> 28 us
  matrix products: 25.1 us -> 0 us
  other arithmetic: 22.6 us -> 2.37 us
  between operations: 13.5 us -> 0.19 us
    psum x1 -> x0, waiting for transfers between devices: 103 us -> none  [spread(): return lax.psum(block, axis)]
    all_gather x1 -> x0, waiting for transfers between devices: 82.1 us -> none  [local(): row_part = lax.all_gather(elements, 'gcol', axis=2, tiled=True)]
    psum x1 -> x0, blocking collectives: 64.6 us -> none  [local(): total_re, total_im = lax.psum((s_re, s_im), ('grow', 'gcol'))]
    ppermute x0 -> x30, starting transfers between devices: none -> 50.7 us  [send(): return lax.ppermute(block, AXES, pairs)]
    ppermute x0 -> x30, waiting for transfers between devices: none -> 30.6 us  [send(): return lax.ppermute(block, AXES, pairs)]
    pallas_call x0 -> x6, Pallas kernels: none -> 28 us  [the longest x4 23.2 us: product(): pl.pallas_call(functools.partial(product_body, z is None, pack, tags), ou...]
    dot_general x1 -> x0, matrix products: 25.1 us -> none  [local(): jnp.einsum('mph,wgh->mpwg', col_part, screened, preferred_element_type=jn...]
    reduce_sum x2 -> x0, other arithmetic: 16.3 us -> none  [the longest x1 16.1 us: local(): s_re = jnp.sum(rre * yre + rim * yim, axis=-1)]
  transfers between devices with their start and end apart: 2 -> 30, of which waited for: 2 -> 14; matrix products, arithmetic and copies ran while one was open for 0% -> 3% of each run, Pallas kernels for 0% -> 22%
where the time goes in v2:
time: 115 us
  starting transfers between devices  50.7 us (44%)
  waiting for transfers between devices  30.6 us (27%)
  Pallas kernels  28 us (24%)
  local copies, waits for them, and re-layouts  2.62 us (2%)
  other arithmetic  2.37 us (2%)
    ppermute x30, starting transfers between devices, send(): return lax.ppermute(block, AXES, pairs)  50.7 us
    ppermute x30, waiting for transfers between devices, send(): return lax.ppermute(block, AXES, pairs)  30.6 us
    pallas_call x4, Pallas kernels, product(): pl.pallas_call(functools.partial(product_body, z is None, pack, tags), ou...  23.2 us
    pallas_call x1, Pallas kernels, form(): pl.pallas_call(functools.partial(form_body, tags), out_shape=jax.ShapeDty...  2.57 us
  transfers between devices with their start and end apart: 30, of which 14 were waited for; matrix products, arithmetic and copies ran while one was open for 3% of the time, Pallas kernels for 22%

profile of v2, /device:TPU:0, one launch (start us, length us, event | category | flops | bytes accessed | tf_op | source)
XLA Modules:
  0.0 114.5 jit_solution(3799715238532201355)
XLA Ops:
  0.0 2.0 %collective-permute-start.2 = (bf16[2,1024,128]{2,1,0:T(8,128)(2,1)}, bf16[2,1024,128]{2,1,0:T(8,128)(2,1)S(1)}, u32[]{:S(2)}, u32[]{:S(2)}) collective-permute-start(bf16[2,1024,128]{2,1,0:T(8,128)(2,1)} %refs_0_.1), channel_id=1, source_target_pairs={{0,4},{1,13},{2,6},{3,15},{4,8},{5,1},{6,10},{7,3},{8,12},{9,5},{1... | collective-permute-start | bytes 1572872 | tf_op jit(solution)/shard_map/ppermute | solution.py:69
  2.0 2.1 %collective-permute-start.3 = (bf16[2,1024,128]{2,1,0:T(8,128)(2,1)}, bf16[2,1024,128]{2,1,0:T(8,128)(2,1)S(1)}, u32[]{:S(2)}, u32[]{:S(2)}) collective-permute-start(bf16[2,1024,128]{2,1,0:T(8,128)(2,1)} %refs_0_.1), channel_id=1, source_target_pairs={{0,12},{1,5},{2,14},{3,7},{4,0},{5,9},{6,2},{7,11},{8,4},{9,13},{1... | collective-permute-start | bytes 1572872 | tf_op jit(solution)/shard_map/ppermute | solution.py:69
  4.1 3.0 %collective-permute-start.1 = (bf16[2,1024,128]{2,1,0:T(8,128)(2,1)}, bf16[2,1024,128]{2,1,0:T(8,128)(2,1)S(1)}, u32[]{:S(2)}, u32[]{:S(2)}) collective-permute-start(bf16[2,1024,128]{2,1,0:T(8,128)(2,1)} %refs_0_.1), channel_id=1, source_target_pairs={{0,2},{1,3},{2,0},{3,1},{4,6},{5,7},{6,4},{7,5},{8,10},{9,11},{10,... | collective-permute-start | bytes 1572872 | tf_op jit(solution)/shard_map/ppermute | solution.py:69
  7.1 3.2 %collective-permute-start = (bf16[2,1024,128]{2,1,0:T(8,128)(2,1)}, bf16[2,1024,128]{2,1,0:T(8,128)(2,1)S(1)}, u32[]{:S(2)}, u32[]{:S(2)}) collective-permute-start(bf16[2,1024,128]{2,1,0:T(8,128)(2,1)} %refs_0_.1), channel_id=1, source_target_pairs={{0,32},{1,0},{2,80},{3,112},{4,16},{5,48},{6,64},{7,96},{8,33},{9,... | collective-permute-start | bytes 1572872 | tf_op jit(solution)/shard_map/ppermute | solution.py:69
  10.3 0.9 select_reduce_fusion.1
  11.2 0.1 copy.10
  11.3 0.1 sub.32
  11.4 0.9 select_reduce_fusion
  12.4 1.4 %copy.11.w_ref = f32[2,1024,16]{2,1,0:T(8,128)} copy(f32[2,1024,16]{1,2,0:T(8,128)S(1)} %pad_maximum_fusion) | data formatting | bytes 262144 | tf_op jit(solution)/shard_map/stack | solution.py:91
  13.7 2.2 %shard_map.55.refs_9_ = f32[2,1024,16]{2,1,0:T(8,128)} custom-call(f32[2,1024,16]{2,1,0:T(8,128)} %copy.11.w_ref), custom_call_target="tpu_custom_call" | custom-call | tf_op jit(solution)/shard_map/pallas_call | solution.py:107
  16.0 3.3 %collective-permute-done.2.refs_1_ = bf16[2,1024,128]{2,1,0:T(8,128)(2,1)S(1)} collective-permute-done((bf16[2,1024,128]{2,1,0:T(8,128)(2,1)}, bf16[2,1024,128]{2,1,0:T(8,128)(2,1)S(1)}, u32[]{:S(2)}, u32[]{:S(2)}) %collective-permute-start.2) | collective-permute-done | bytes 524320 | tf_op jit(solution)/shard_map/ppermute | solution.py:69
  19.2 1.1 collective-permute-start.5
  20.4 0.0 collective-permute-start.6
  20.4 0.0 collective-permute-done.1.refs_3_
  20.4 0.5 collective-permute-start.7
  20.9 0.0 collective-permute-done.refs_0_
  20.9 0.0 collective-permute-done.4.refs_0_
  20.9 1.0 collective-permute-done.5.refs_1_
  21.9 0.7 collective-permute-done.6.refs_2_
  22.7 0.7 collective-permute-done.7.refs_3_
  23.4 2.1 %collective-permute-start.12 = (bf16[2,1024,128]{2,1,0:T(8,128)(2,1)S(1)}, bf16[2,1024,128]{2,1,0:T(8,128)(2,1)S(1)}, u32[]{:S(2)}, u32[]{:S(2)}) collective-permute-start(bf16[2,1024,128]{2,1,0:T(8,128)(2,1)S(1)} %collective-permute-done.2.refs_1_), channel_id=1, source_target_pairs={{0,4},{1,13},{2,6},{3,15},{4,8},{5,1},{6,10},{7,3},{8,12},{9,5},{1... | collective-permute-start | bytes 1572872 | tf_op jit(solution)/shard_map/ppermute | solution.py:69
  25.5 3.3 %collective-permute-start.10 = (bf16[2,1024,128]{2,1,0:T(8,128)(2,1)S(1)}, bf16[2,1024,128]{2,1,0:T(8,128)(2,1)S(1)}, u32[]{:S(2)}, u32[]{:S(2)}) collective-permute-start(bf16[2,1024,128]{2,1,0:T(8,128)(2,1)S(1)} %collective-permute-done.refs_0_), channel_id=1, source_target_pairs={{0,32},{1,33},{2,34},{3,35},{4,36},{5,37},{6,38},{7,39},{8,40},{9,... | collective-permute-start | bytes 1572872 | tf_op jit(solution)/shard_map/ppermute | solution.py:69
  28.8 7.3 %collective-permute-start.11 = (bf16[2,1024,128]{2,1,0:T(8,128)(2,1)S(1)}, bf16[2,1024,128]{2,1,0:T(8,128)(2,1)S(1)}, u32[]{:S(2)}, u32[]{:S(2)}) collective-permute-start(bf16[2,1024,128]{2,1,0:T(8,128)(2,1)S(1)} %collective-permute-done.refs_0_), channel_id=1, source_target_pairs={{0,64},{1,65},{2,66},{3,67},{4,68},{5,69},{6,70},{7,71},{8,72},{9,... | collective-permute-start | bytes 1572872 | tf_op jit(solution)/shard_map/ppermute | solution.py:69
  36.1 0.0 collective-permute-start.8
  36.1 3.2 %collective-permute-start.9 = (bf16[2,1024,128]{2,1,0:T(8,128)(2,1)S(1)}, bf16[2,1024,128]{2,1,0:T(8,128)(2,1)S(1)}, u32[]{:S(2)}, u32[]{:S(2)}) collective-permute-start(bf16[2,1024,128]{2,1,0:T(8,128)(2,1)S(1)} %collective-permute-done.refs_0_), channel_id=1, source_target_pairs={{0,48},{1,17},{2,50},{3,19},{4,52},{5,21},{6,54},{7,23},{8,56},{9,... | collective-permute-start | bytes 1572872 | tf_op jit(solution)/shard_map/ppermute | solution.py:69
  39.3 3.0 %collective-permute-done.12.refs_0_ = bf16[2,1024,128]{2,1,0:T(8,128)(2,1)S(1)} collective-permute-done((bf16[2,1024,128]{2,1,0:T(8,128)(2,1)S(1)}, bf16[2,1024,128]{2,1,0:T(8,128)(2,1)S(1)}, u32[]{:S(2)}, u32[]{:S(2)}) %collective-permute-start.12) | collective-permute-done | bytes 524320 | tf_op jit(solution)/shard_map/ppermute | solution.py:69
  42.3 0.0 collective-permute-start.14
  42.4 0.0 collective-permute-done.10.refs_2_
  42.4 9.3 %collective-permute-start.15 = (bf16[2,1024,128]{2,1,0:T(8,128)(2,1)S(1)}, bf16[2,1024,128]{2,1,0:T(8,128)(2,1)S(1)}, u32[]{:S(2)}, u32[]{:S(2)}) collective-permute-start(bf16[2,1024,128]{2,1,0:T(8,128)(2,1)S(1)} %collective-permute-done.1.refs_3_), channel_id=1, source_target_pairs={{0,12},{1,5},{2,14},{3,7},{4,0},{5,9},{6,2},{7,11},{8,4},{9,13},{1... | collective-permute-start | bytes 1572872 | tf_op jit(solution)/shard_map/ppermute | solution.py:69
  51.6 3.5 %collective-permute-start.13 = (bf16[2,1024,128]{2,1,0:T(8,128)(2,1)S(1)}, bf16[2,1024,128]{2,1,0:T(8,128)(2,1)S(1)}, u32[]{:S(2)}, u32[]{:S(2)}) collective-permute-start(bf16[2,1024,128]{2,1,0:T(8,128)(2,1)S(1)} %collective-permute-done.12.refs_0_), channel_id=1, source_target_pairs={{0,2},{1,3},{2,0},{3,1},{4,6},{5,7},{6,4},{7,5},{8,10},{9,11},{10,... | collective-permute-start | bytes 1572872 | tf_op jit(solution)/shard_map/ppermute | solution.py:69
  55.1 1.0 copy-done.1
  56.1 5.8 %shard_map.56.refs_5_ = f32[2,1024,1024]{2,1,0:T(8,128)S(1)} custom-call(bf16[2,1024,128]{2,1,0:T(8,128)(2,1)S(1)} %copy-done.1, bf16[2,1024,128]{2,1,0:T(8,128)(2,1)S(1)} %collective-permute-done.2.refs_1_, bf16[2,1024,128]{2,1,0:T(8,128)(2,1)S(1)} %collective-permute-done.3.refs_2_, bf16[2,1024,128]{2,1,0:T(8,128)(2,1)S(1)} %collective-permute-done.1.refs_3_, ...), custom_call_target="tpu_custom_call" | custom-call | flops 1 | bytes 1 | tf_op jit(solution)/shard_map/pallas_call | solution.py:179
  61.9 5.8 %shard_map.57.refs_5_ = f32[2,1024,1024]{2,1,0:T(8,128)S(1)} custom-call(bf16[2,1024,128]{2,1,0:T(8,128)(2,1)S(1)} %collective-permute-done.4.refs_0_, bf16[2,1024,128]{2,1,0:T(8,128)(2,1)S(1)} %collective-permute-done.5.refs_1_, bf16[2,1024,128]{2,1,0:T(8,128)(2,1)S(1)} %collective-permute-done.6.refs_2_, ...), custom_call_target="tpu_custom_call", output_to_operand_aliasing={{}: (5, {})} | custom-call | flops 1 | bytes 1 | tf_op jit(solution)/shard_map/pallas_call | solution.py:179
  67.7 0.0 collective-permute-done.8.refs_1_
  67.7 0.0 collective-permute-done.14.refs_1_
  67.7 0.0 collective-permute-done.15.refs_3_
  67.8 0.1 collective-permute-start.19
  67.9 0.5 collective-permute-start.20
  68.3 0.1 collective-permute-start.21
  68.4 0.4 collective-permute-start.22
  68.9 0.3 collective-permute-start.16
  69.2 0.5 collective-permute-done.19.refs_0_
  69.7 2.4 %collective-permute-start.17 = (bf16[2,1024,128]{2,1,0:T(8,128)(2,1)S(1)}, bf16[2,1024,128]{2,1,0:T(8,128)(2,1)S(1)}, u32[]{:S(2)}, u32[]{:S(2)}) collective-permute-start(bf16[2,1024,128]{2,1,0:T(8,128)(2,1)S(1)} %collective-permute-done.11.refs_4_), channel_id=1, source_target_pairs={{0,48},{1,17},{2,50},{3,19},{4,52},{5,21},{6,54},{7,23},{8,56},{9,... | collective-permute-start | bytes 1572872 | tf_op jit(solution)/shard_map/ppermute | solution.py:69
  72.1 0.0 collective-permute-start.18
  72.1 5.8 %shard_map.58.refs_5_ = f32[2,1024,1024]{2,1,0:T(8,128)S(1)} custom-call(bf16[2,1024,128]{2,1,0:T(8,128)(2,1)S(1)} %collective-permute-done.12.refs_0_, bf16[2,1024,128]{2,1,0:T(8,128)(2,1)S(1)} %collective-permute-done.14.refs_1_, bf16[2,1024,128]{2,1,0:T(8,128)(2,1)S(1)} %collective-permute-done.13.refs_2_, ...), custom_call_target="tpu_custom_call", output_to_operand_aliasing={{}: (5, {})} | custom-call | flops 1 | bytes 1 | tf_op jit(solution)/shard_map/pallas_call | solution.py:179
  77.9 0.0 collective-permute-done.21.refs_2_
  77.9 5.9 %shard_map.59.refs_8_ = f32[2,1024,1024]{2,1,0:T(8,128)S(1)} custom-call(bf16[2,1024,128]{2,1,0:T(8,128)(2,1)S(1)} %collective-permute-done.19.refs_0_, bf16[2,1024,128]{2,1,0:T(8,128)(2,1)S(1)} %collective-permute-done.20.refs_1_, bf16[2,1024,128]{2,1,0:T(8,128)(2,1)S(1)} %collective-permute-done.21.refs_2_, ...), custom_call_target="tpu_custom_call", output_to_operand_aliasing={{}: (5, {})} | custom-call | flops 1 | bytes 1 | tf_op jit(solution)/shard_map/pallas_call | solution.py:179
  83.8 1.0 collective-permute-done.16.refs_5_
  84.8 2.6 %shard_map.60 = f32[2,4,16]{2,1,0:T(4,128)S(1)} custom-call(bf16[2,1024,128]{2,1,0:T(8,128)(2,1)S(1)} %collective-permute-done.refs_0_, bf16[2,1024,128]{2,1,0:T(8,128)(2,1)S(1)} %collective-permute-done.8.refs_1_, bf16[2,1024,128]{2,1,0:T(8,128)(2,1)S(1)} %collective-permute-done.10.refs_2_, bf16[2,1024,128]{2,1,0:T(8,128)(2,1)S(1)} %collective-permute-done.9.refs_3_, ...), custom_call_target="tpu_custom_call" | custom-call | flops 1 | bytes 1 | tf_op jit(solution)/shard_map/pallas_call | solution.py:239
  87.4 0.2 collective-permute-start.23
  87.6 1.1 collective-permute-done.23
  88.6 1.0 collective-permute-start.24
  89.7 2.6 %collective-permute-done.24 = f32[2,4,16]{2,1,0:T(4,128)S(1)} collective-permute-done((f32[2,4,16]{2,1,0:T(4,128)S(1)}, f32[2,4,16]{2,1,0:T(4,128)S(1)}, u32[]{:S(2)}, u32[]{:S(2)}) %collective-permute-start.24) | collective-permute-done | bytes 544 | tf_op jit(solution)/shard_map/ppermute | solution.py:69
  92.2 1.0 collective-permute-start.25
  93.2 3.8 %collective-permute-done.25 = f32[2,4,16]{2,1,0:T(4,128)S(1)} collective-permute-done((f32[2,4,16]{2,1,0:T(4,128)S(1)}, f32[2,4,16]{2,1,0:T(4,128)S(1)}, u32[]{:S(2)}, u32[]{:S(2)}) %collective-permute-start.25) | collective-permute-done | bytes 544 | tf_op jit(solution)/shard_map/ppermute | solution.py:69
  97.1 0.0 collective-permute-start.26
  97.1 3.6 %collective-permute-done.26 = f32[2,4,16]{2,1,0:T(4,128)S(1)} collective-permute-done((f32[2,4,16]{2,1,0:T(4,128)S(1)}, f32[2,4,16]{2,1,0:T(4,128)S(1)}, u32[]{:S(2)}, u32[]{:S(2)}) %collective-permute-start.26) | collective-permute-done | bytes 544 | tf_op jit(solution)/shard_map/ppermute | solution.py:69
  100.7 1.9 %collective-permute-start.27 = (f32[2,4,16]{2,1,0:T(4,128)S(1)}, f32[2,4,16]{2,1,0:T(4,128)S(1)}, u32[]{:S(2)}, u32[]{:S(2)}) collective-permute-start(f32[2,4,16]{2,1,0:T(4,128)S(1)} %add.45), channel_id=1, source_target_pairs={{0,48},{1,49},{2,50},{3,51},{4,52},{5,53},{6,54},{7,55},{8,56},{9,... | collective-permute-start | bytes 1544 | tf_op jit(solution)/shard_map/ppermute | solution.py:69
  102.5 3.0 %collective-permute-done.27 = f32[2,4,16]{2,1,0:T(4,128)S(1)} collective-permute-done((f32[2,4,16]{2,1,0:T(4,128)S(1)}, f32[2,4,16]{2,1,0:T(4,128)S(1)}, u32[]{:S(2)}, u32[]{:S(2)}) %collective-permute-start.27) | collective-permute-done | bytes 544 | tf_op jit(solution)/shard_map/ppermute | solution.py:69
  105.5 0.3 collective-permute-start.28
  105.8 3.3 %collective-permute-done.28 = f32[2,4,16]{2,1,0:T(4,128)S(1)} collective-permute-done((f32[2,4,16]{2,1,0:T(4,128)S(1)}, f32[2,4,16]{2,1,0:T(4,128)S(1)}, u32[]{:S(2)}, u32[]{:S(2)}) %collective-permute-start.28) | collective-permute-done | bytes 544 | tf_op jit(solution)/shard_map/ppermute | solution.py:69
  109.1 2.0 %collective-permute-start.29 = (f32[2,4,16]{2,1,0:T(4,128)S(1)}, f32[2,4,16]{2,1,0:T(4,128)S(1)}, u32[]{:S(2)}, u32[]{:S(2)}) collective-permute-start(f32[2,4,16]{2,1,0:T(4,128)S(1)} %add.47), channel_id=1, source_target_pairs={{0,12},{1,13},{2,14},{3,15},{4,8},{5,9},{6,10},{7,11},{8,4},{9,5},... | collective-permute-start | bytes 1544 | tf_op jit(solution)/shard_map/ppermute | solution.py:69
  111.1 2.9 %collective-permute-done.29 = f32[2,4,16]{2,1,0:T(4,128)S(1)} collective-permute-done((f32[2,4,16]{2,1,0:T(4,128)S(1)}, f32[2,4,16]{2,1,0:T(4,128)S(1)}, u32[]{:S(2)}, u32[]{:S(2)}) %collective-permute-start.29) | collective-permute-done | bytes 544 | tf_op jit(solution)/shard_map/ppermute | solution.py:69
  113.9 0.6 add.48
  (23 shorter events, 0.1 us)
Async XLA Ops:
  0.0 19.2 %collective-permute-start.2 = (bf16[2,1024,128]{2,1,0:T(8,128)(2,1)}, bf16[2,1024,128]{2,1,0:T(8,128)(2,1)S(1)}, u32[]{:S(2)}, u32[]{:S(2)}) collective-permute-start(bf16[2,1024,128]{2,1,0:T(8,128)(2,1)} %refs_0_.1), channel_id=1, source_target_pairs={{0,4},{1,13},{2,6},{3,15},{4,8},{5,1},{6,10},{7,3},{8,12},{9,5},{1... | collective-permute-start | bytes 1572872 | tf_op jit(solution)/shard_map/ppermute | solution.py:69
  2.0 17.2 %collective-permute-start.3 = (bf16[2,1024,128]{2,1,0:T(8,128)(2,1)}, bf16[2,1024,128]{2,1,0:T(8,128)(2,1)S(1)}, u32[]{:S(2)}, u32[]{:S(2)}) collective-permute-start(bf16[2,1024,128]{2,1,0:T(8,128)(2,1)} %refs_0_.1), channel_id=1, source_target_pairs={{0,12},{1,5},{2,14},{3,7},{4,0},{5,9},{6,2},{7,11},{8,4},{9,13},{1... | collective-permute-start | bytes 1572872 | tf_op jit(solution)/shard_map/ppermute | solution.py:69
  4.1 16.3 %collective-permute-start.1 = (bf16[2,1024,128]{2,1,0:T(8,128)(2,1)}, bf16[2,1024,128]{2,1,0:T(8,128)(2,1)S(1)}, u32[]{:S(2)}, u32[]{:S(2)}) collective-permute-start(bf16[2,1024,128]{2,1,0:T(8,128)(2,1)} %refs_0_.1), channel_id=1, source_target_pairs={{0,2},{1,3},{2,0},{3,1},{4,6},{5,7},{6,4},{7,5},{8,10},{9,11},{10,... | collective-permute-start | bytes 1572872 | tf_op jit(solution)/shard_map/ppermute | solution.py:69
  7.1 13.7 %collective-permute-start = (bf16[2,1024,128]{2,1,0:T(8,128)(2,1)}, bf16[2,1024,128]{2,1,0:T(8,128)(2,1)S(1)}, u32[]{:S(2)}, u32[]{:S(2)}) collective-permute-start(bf16[2,1024,128]{2,1,0:T(8,128)(2,1)} %refs_0_.1), channel_id=1, source_target_pairs={{0,32},{1,0},{2,80},{3,112},{4,16},{5,48},{6,64},{7,96},{8,33},{9,... | collective-permute-start | bytes 1572872 | tf_op jit(solution)/shard_map/ppermute | solution.py:69
  10.3 10.5 %collective-permute-start.4 = (bf16[2,1024,128]{2,1,0:T(8,128)(2,1)}, bf16[2,1024,128]{2,1,0:T(8,128)(2,1)S(1)}, u32[]{:S(2)}, u32[]{:S(2)}) collective-permute-start(bf16[2,1024,128]{2,1,0:T(8,128)(2,1)} %refs_0_.1), channel_id=1, source_target_pairs={{0,1},{1,0},{2,3},{3,2},{4,5},{5,4},{6,7},{7,6},{8,9},{9,8},{10,11... | collective-permute-start | bytes 1572872 | tf_op jit(solution)/shard_map/ppermute | solution.py:69
  19.2 2.7 %collective-permute-start.5 = (bf16[2,1024,128]{2,1,0:T(8,128)(2,1)S(1)}, bf16[2,1024,128]{2,1,0:T(8,128)(2,1)S(1)}, u32[]{:S(2)}, u32[]{:S(2)}) collective-permute-start(bf16[2,1024,128]{2,1,0:T(8,128)(2,1)S(1)} %collective-permute-done.2.refs_1_), channel_id=1, source_target_pairs={{0,1},{1,0},{2,3},{3,2},{4,5},{5,4},{6,7},{7,6},{8,9},{9,8},{10,11... | collective-permute-start | bytes 1572872 | tf_op jit(solution)/shard_map/ppermute | solution.py:69
  20.4 2.3 %collective-permute-start.6 = (bf16[2,1024,128]{2,1,0:T(8,128)(2,1)S(1)}, bf16[2,1024,128]{2,1,0:T(8,128)(2,1)S(1)}, u32[]{:S(2)}, u32[]{:S(2)}) collective-permute-start(bf16[2,1024,128]{2,1,0:T(8,128)(2,1)S(1)} %collective-permute-done.3.refs_2_), channel_id=1, source_target_pairs={{0,1},{1,0},{2,3},{3,2},{4,5},{5,4},{6,7},{7,6},{8,9},{9,8},{10,11... | collective-permute-start | bytes 1572872 | tf_op jit(solution)/shard_map/ppermute | solution.py:69
  20.4 3.0 %collective-permute-start.7 = (bf16[2,1024,128]{2,1,0:T(8,128)(2,1)S(1)}, bf16[2,1024,128]{2,1,0:T(8,128)(2,1)S(1)}, u32[]{:S(2)}, u32[]{:S(2)}) collective-permute-start(bf16[2,1024,128]{2,1,0:T(8,128)(2,1)S(1)} %collective-permute-done.1.refs_3_), channel_id=1, source_target_pairs={{0,1},{1,0},{2,3},{3,2},{4,5},{5,4},{6,7},{7,6},{8,9},{9,8},{10,11... | collective-permute-start | bytes 1572872 | tf_op jit(solution)/shard_map/ppermute | solution.py:69
  23.4 18.9 %collective-permute-start.12 = (bf16[2,1024,128]{2,1,0:T(8,128)(2,1)S(1)}, bf16[2,1024,128]{2,1,0:T(8,128)(2,1)S(1)}, u32[]{:S(2)}, u32[]{:S(2)}) collective-permute-start(bf16[2,1024,128]{2,1,0:T(8,128)(2,1)S(1)} %collective-permute-done.2.refs_1_), channel_id=1, source_target_pairs={{0,4},{1,13},{2,6},{3,15},{4,8},{5,1},{6,10},{7,3},{8,12},{9,5},{1... | collective-permute-start | bytes 1572872 | tf_op jit(solution)/shard_map/ppermute | solution.py:69
  25.5 16.9 %collective-permute-start.10 = (bf16[2,1024,128]{2,1,0:T(8,128)(2,1)S(1)}, bf16[2,1024,128]{2,1,0:T(8,128)(2,1)S(1)}, u32[]{:S(2)}, u32[]{:S(2)}) collective-permute-start(bf16[2,1024,128]{2,1,0:T(8,128)(2,1)S(1)} %collective-permute-done.refs_0_), channel_id=1, source_target_pairs={{0,32},{1,33},{2,34},{3,35},{4,36},{5,37},{6,38},{7,39},{8,40},{9,... | collective-permute-start | bytes 1572872 | tf_op jit(solution)/shard_map/ppermute | solution.py:69
  28.8 22.8 %collective-permute-start.11 = (bf16[2,1024,128]{2,1,0:T(8,128)(2,1)S(1)}, bf16[2,1024,128]{2,1,0:T(8,128)(2,1)S(1)}, u32[]{:S(2)}, u32[]{:S(2)}) collective-permute-start(bf16[2,1024,128]{2,1,0:T(8,128)(2,1)S(1)} %collective-permute-done.refs_0_), channel_id=1, source_target_pairs={{0,64},{1,65},{2,66},{3,67},{4,68},{5,69},{6,70},{7,71},{8,72},{9,... | collective-permute-start | bytes 1572872 | tf_op jit(solution)/shard_map/ppermute | solution.py:69
  36.1 31.6 %collective-permute-start.8 = (bf16[2,1024,128]{2,1,0:T(8,128)(2,1)S(1)}, bf16[2,1024,128]{2,1,0:T(8,128)(2,1)S(1)}, u32[]{:S(2)}, u32[]{:S(2)}) collective-permute-start(bf16[2,1024,128]{2,1,0:T(8,128)(2,1)S(1)} %collective-permute-done.refs_0_), channel_id=1, source_target_pairs={{0,16},{1,49},{2,18},{3,51},{4,20},{5,53},{6,22},{7,55},{8,24},{9,... | collective-permute-start | bytes 1572872 | tf_op jit(solution)/shard_map/ppermute | solution.py:69
  36.1 31.6 %collective-permute-start.9 = (bf16[2,1024,128]{2,1,0:T(8,128)(2,1)S(1)}, bf16[2,1024,128]{2,1,0:T(8,128)(2,1)S(1)}, u32[]{:S(2)}, u32[]{:S(2)}) collective-permute-start(bf16[2,1024,128]{2,1,0:T(8,128)(2,1)S(1)} %collective-permute-done.refs_0_), channel_id=1, source_target_pairs={{0,48},{1,17},{2,50},{3,19},{4,52},{5,21},{6,54},{7,23},{8,56},{9,... | collective-permute-start | bytes 1572872 | tf_op jit(solution)/shard_map/ppermute | solution.py:69
  42.3 25.4 %collective-permute-start.14 = (bf16[2,1024,128]{2,1,0:T(8,128)(2,1)S(1)}, bf16[2,1024,128]{2,1,0:T(8,128)(2,1)S(1)}, u32[]{:S(2)}, u32[]{:S(2)}) collective-permute-start(bf16[2,1024,128]{2,1,0:T(8,128)(2,1)S(1)} %collective-permute-done.1.refs_3_), channel_id=1, source_target_pairs={{0,4},{1,13},{2,6},{3,15},{4,8},{5,1},{6,10},{7,3},{8,12},{9,5},{1... | collective-permute-start | bytes 1572872 | tf_op jit(solution)/shard_map/ppermute | solution.py:69
  42.4 25.4 %collective-permute-start.15 = (bf16[2,1024,128]{2,1,0:T(8,128)(2,1)S(1)}, bf16[2,1024,128]{2,1,0:T(8,128)(2,1)S(1)}, u32[]{:S(2)}, u32[]{:S(2)}) collective-permute-start(bf16[2,1024,128]{2,1,0:T(8,128)(2,1)S(1)} %collective-permute-done.1.refs_3_), channel_id=1, source_target_pairs={{0,12},{1,5},{2,14},{3,7},{4,0},{5,9},{6,2},{7,11},{8,4},{9,13},{1... | collective-permute-start | bytes 1572872 | tf_op jit(solution)/shard_map/ppermute | solution.py:69
  51.6 16.1 %collective-permute-start.13 = (bf16[2,1024,128]{2,1,0:T(8,128)(2,1)S(1)}, bf16[2,1024,128]{2,1,0:T(8,128)(2,1)S(1)}, u32[]{:S(2)}, u32[]{:S(2)}) collective-permute-start(bf16[2,1024,128]{2,1,0:T(8,128)(2,1)S(1)} %collective-permute-done.12.refs_0_), channel_id=1, source_target_pairs={{0,2},{1,3},{2,0},{3,1},{4,6},{5,7},{6,4},{7,5},{8,10},{9,11},{10,... | collective-permute-start | bytes 1572872 | tf_op jit(solution)/shard_map/ppermute | solution.py:69
  55.1 1.0 copy-start.1
  67.8 2.0 %collective-permute-start.19 = (bf16[2,1024,128]{2,1,0:T(8,128)(2,1)S(1)}, bf16[2,1024,128]{2,1,0:T(8,128)(2,1)S(1)}, u32[]{:S(2)}, u32[]{:S(2)}) collective-permute-start(bf16[2,1024,128]{2,1,0:T(8,128)(2,1)S(1)} %collective-permute-done.12.refs_0_), channel_id=1, source_target_pairs={{0,1},{1,0},{2,3},{3,2},{4,5},{5,4},{6,7},{7,6},{8,9},{9,8},{10,11... | collective-permute-start | bytes 1572872 | tf_op jit(solution)/shard_map/ppermute | solution.py:69
  67.9 4.3 %collective-permute-start.20 = (bf16[2,1024,128]{2,1,0:T(8,128)(2,1)S(1)}, bf16[2,1024,128]{2,1,0:T(8,128)(2,1)S(1)}, u32[]{:S(2)}, u32[]{:S(2)}) collective-permute-start(bf16[2,1024,128]{2,1,0:T(8,128)(2,1)S(1)} %collective-permute-done.14.refs_1_), channel_id=1, source_target_pairs={{0,1},{1,0},{2,3},{3,2},{4,5},{5,4},{6,7},{7,6},{8,9},{9,8},{10,11... | collective-permute-start | bytes 1572872 | tf_op jit(solution)/shard_map/ppermute | solution.py:69
  68.3 9.6 %collective-permute-start.21 = (bf16[2,1024,128]{2,1,0:T(8,128)(2,1)S(1)}, bf16[2,1024,128]{2,1,0:T(8,128)(2,1)S(1)}, u32[]{:S(2)}, u32[]{:S(2)}) collective-permute-start(bf16[2,1024,128]{2,1,0:T(8,128)(2,1)S(1)} %collective-permute-done.13.refs_2_), channel_id=1, source_target_pairs={{0,1},{1,0},{2,3},{3,2},{4,5},{5,4},{6,7},{7,6},{8,9},{9,8},{10,11... | collective-permute-start | bytes 1572872 | tf_op jit(solution)/shard_map/ppermute | solution.py:69
  68.4 9.5 %collective-permute-start.22 = (bf16[2,1024,128]{2,1,0:T(8,128)(2,1)S(1)}, bf16[2,1024,128]{2,1,0:T(8,128)(2,1)S(1)}, u32[]{:S(2)}, u32[]{:S(2)}) collective-permute-start(bf16[2,1024,128]{2,1,0:T(8,128)(2,1)S(1)} %collective-permute-done.15.refs_3_), channel_id=1, source_target_pairs={{0,1},{1,0},{2,3},{3,2},{4,5},{5,4},{6,7},{7,6},{8,9},{9,8},{10,11... | collective-permute-start | bytes 1572872 | tf_op jit(solution)/shard_map/ppermute | solution.py:69
  68.9 15.9 %collective-permute-start.16 = (bf16[2,1024,128]{2,1,0:T(8,128)(2,1)S(1)}, bf16[2,1024,128]{2,1,0:T(8,128)(2,1)S(1)}, u32[]{:S(2)}, u32[]{:S(2)}) collective-permute-start(bf16[2,1024,128]{2,1,0:T(8,128)(2,1)S(1)} %collective-permute-done.11.refs_4_), channel_id=1, source_target_pairs={{0,16},{1,49},{2,18},{3,51},{4,20},{5,53},{6,22},{7,55},{8,24},{9,... | collective-permute-start | bytes 1572872 | tf_op jit(solution)/shard_map/ppermute | solution.py:69
  69.7 15.1 %collective-permute-start.17 = (bf16[2,1024,128]{2,1,0:T(8,128)(2,1)S(1)}, bf16[2,1024,128]{2,1,0:T(8,128)(2,1)S(1)}, u32[]{:S(2)}, u32[]{:S(2)}) collective-permute-start(bf16[2,1024,128]{2,1,0:T(8,128)(2,1)S(1)} %collective-permute-done.11.refs_4_), channel_id=1, source_target_pairs={{0,48},{1,17},{2,50},{3,19},{4,52},{5,21},{6,54},{7,23},{8,56},{9,... | collective-permute-start | bytes 1572872 | tf_op jit(solution)/shard_map/ppermute | solution.py:69
  72.1 12.7 %collective-permute-start.18 = (bf16[2,1024,128]{2,1,0:T(8,128)(2,1)S(1)}, bf16[2,1024,128]{2,1,0:T(8,128)(2,1)S(1)}, u32[]{:S(2)}, u32[]{:S(2)}) collective-permute-start(bf16[2,1024,128]{2,1,0:T(8,128)(2,1)S(1)} %collective-permute-done.10.refs_2_), channel_id=1, source_target_pairs={{0,64},{1,65},{2,66},{3,67},{4,68},{5,69},{6,70},{7,71},{8,72},{9,... | collective-permute-start | bytes 1572872 | tf_op jit(solution)/shard_map/ppermute | solution.py:69
  77.9 6.9 %copy-start = (f32[2,1024,16]{2,1,0:T(8,128)S(1)}, f32[2,1024,16]{2,1,0:T(8,128)}, u32[]{:S(2)}) copy-start(f32[2,1024,16]{2,1,0:T(8,128)} %shard_map.55.refs_9_) | copy-start | bytes 393220
  87.4 1.2 %collective-permute-start.23 = (f32[2,4,16]{2,1,0:T(4,128)S(1)}, f32[2,4,16]{2,1,0:T(4,128)S(1)}, u32[]{:S(2)}, u32[]{:S(2)}) collective-permute-start(f32[2,4,16]{2,1,0:T(4,128)S(1)} %shard_map.60), channel_id=1, source_target_pairs={{0,1},{1,0},{2,3},{3,2},{4,5},{5,4},{6,7},{7,6},{8,9},{9,8},{10,11... | collective-permute-start | bytes 1544 | tf_op jit(solution)/shard_map/ppermute | solution.py:69
  88.6 3.6 %collective-permute-start.24 = (f32[2,4,16]{2,1,0:T(4,128)S(1)}, f32[2,4,16]{2,1,0:T(4,128)S(1)}, u32[]{:S(2)}, u32[]{:S(2)}) collective-permute-start(f32[2,4,16]{2,1,0:T(4,128)S(1)} %add.42), channel_id=1, source_target_pairs={{0,64},{1,65},{2,66},{3,67},{4,68},{5,69},{6,70},{7,71},{8,72},{9,... | collective-permute-start | bytes 1544 | tf_op jit(solution)/shard_map/ppermute | solution.py:69
  92.2 4.8 %collective-permute-start.25 = (f32[2,4,16]{2,1,0:T(4,128)S(1)}, f32[2,4,16]{2,1,0:T(4,128)S(1)}, u32[]{:S(2)}, u32[]{:S(2)}) collective-permute-start(f32[2,4,16]{2,1,0:T(4,128)S(1)} %add.43), channel_id=1, source_target_pairs={{0,66},{1,67},{2,64},{3,65},{4,70},{5,71},{6,68},{7,69},{8,74},{9,... | collective-permute-start | bytes 1544 | tf_op jit(solution)/shard_map/ppermute | solution.py:69
  97.1 3.6 %collective-permute-start.26 = (f32[2,4,16]{2,1,0:T(4,128)S(1)}, f32[2,4,16]{2,1,0:T(4,128)S(1)}, u32[]{:S(2)}, u32[]{:S(2)}) collective-permute-start(f32[2,4,16]{2,1,0:T(4,128)S(1)} %add.44), channel_id=1, source_target_pairs={{0,16},{1,17},{2,18},{3,19},{4,20},{5,21},{6,22},{7,23},{8,24},{9,... | collective-permute-start | bytes 1544 | tf_op jit(solution)/shard_map/ppermute | solution.py:69
  100.7 4.8 %collective-permute-start.27 = (f32[2,4,16]{2,1,0:T(4,128)S(1)}, f32[2,4,16]{2,1,0:T(4,128)S(1)}, u32[]{:S(2)}, u32[]{:S(2)}) collective-permute-start(f32[2,4,16]{2,1,0:T(4,128)S(1)} %add.45), channel_id=1, source_target_pairs={{0,48},{1,49},{2,50},{3,51},{4,52},{5,53},{6,54},{7,55},{8,56},{9,... | collective-permute-start | bytes 1544 | tf_op jit(solution)/shard_map/ppermute | solution.py:69
  105.5 3.6 %collective-permute-start.28 = (f32[2,4,16]{2,1,0:T(4,128)S(1)}, f32[2,4,16]{2,1,0:T(4,128)S(1)}, u32[]{:S(2)}, u32[]{:S(2)}) collective-permute-start(f32[2,4,16]{2,1,0:T(4,128)S(1)} %add.46), channel_id=1, source_target_pairs={{0,4},{1,5},{2,6},{3,7},{4,0},{5,1},{6,2},{7,3},{8,12},{9,13},{10,... | collective-permute-start | bytes 1544 | tf_op jit(solution)/shard_map/ppermute | solution.py:69
  109.1 4.8 %collective-permute-start.29 = (f32[2,4,16]{2,1,0:T(4,128)S(1)}, f32[2,4,16]{2,1,0:T(4,128)S(1)}, u32[]{:S(2)}, u32[]{:S(2)}) collective-permute-start(f32[2,4,16]{2,1,0:T(4,128)S(1)} %add.47), channel_id=1, source_target_pairs={{0,12},{1,13},{2,14},{3,15},{4,8},{5,9},{6,10},{7,11},{8,4},{9,5},... | collective-permute-start | bytes 1544 | tf_op jit(solution)/shard_map/ppermute | solution.py:69

commit v3 on v2

--- a/solution.py
+++ b/solution.py
@@ -261,11 +261,11 @@
     u0 = send(t0, X_NEAR)
     n2 = send(n1, Z_ON)
     z, = product(((0, 0, False), (0, 1, False), (0, 3, False), (1, 0, False)), [elements, n1, n3, p0], screened)
-    p2 = send(n2, X_FAR)
+    p2 = send(after(n2, z), X_FAR)
     late = after(p0, n2)
     p1, p3 = send(late, Z_ON), send(late, Z_BACK)
     z, = product(((0, 0, True), (0, 1, True), (0, 3, True), (1, 0, True)), [m0, m1, m3, q0], screened, z)
-    t1, t3, t2, u0, n2, p2, p1, p3, z = meet(t1, t3, t2, u0, n2, p2, p1, p3, z)
+    t1, t3, t2, u0 = meet(t1, t3, t2, u0)
 
     u1, u3, u2 = send(u0, Y_ON), send(u0, Y_BACK), send(t2, X_NEAR)
     m2, q2, q1, q3 = [send(block, CORE) for block in (n2, p2, p1, p3)]

time: 115 us -> 115 us (level)
  starting transfers between devices: 50.7 us -> 46.6 us
  waiting for transfers between devices: 30.6 us -> 34.5 us
    ppermute x30, starting transfers between devices: 50.7 us -> 46.6 us  [send(): return lax.ppermute(block, AXES, pairs)]
    ppermute x30, waiting for transfers between devices: 30.6 us -> 34.5 us  [send(): return lax.ppermute(block, AXES, pairs)]
  transfers between devices with their start and end apart: 30 -> 30, of which waited for: 14 -> 13; matrix products, arithmetic and copies ran while one was open for 3% -> 3% of each run, Pallas kernels for 22% -> 22%
where the time goes in v3:
time: 115 us; the launch traced here: 114 us
  starting transfers between devices  46.6 us (41%)
  waiting for transfers between devices  34.5 us (30%)
  Pallas kernels  28 us (24%)
  local copies, waits for them, and re-layouts  2.62 us (2%)
  other arithmetic  2.37 us (2%)
    ppermute x30, starting transfers between devices, send(): return lax.ppermute(block, AXES, pairs)  46.6 us
    ppermute x30, waiting for transfers between devices, send(): return lax.ppermute(block, AXES, pairs)  34.5 us
    pallas_call x4, Pallas kernels, product(): pl.pallas_call(functools.partial(product_body, z is None, pack, tags), ou...  23.2 us
    pallas_call x1, Pallas kernels, form(): pl.pallas_call(functools.partial(form_body, tags), out_shape=jax.ShapeDty...  2.57 us
  transfers between devices with their start and end apart: 30, of which 13 were waited for; matrix products, arithmetic and copies ran while one was open for 3% of the time, Pallas kernels for 22%

profile of v3, /device:TPU:0, one launch (start us, length us, event | category | flops | bytes accessed | tf_op | source)
XLA Modules:
  0.0 114.3 jit_solution(2654530102155297427)
XLA Ops:
  0.0 2.0 %collective-permute-start.2 = (bf16[2,1024,128]{2,1,0:T(8,128)(2,1)}, bf16[2,1024,128]{2,1,0:T(8,128)(2,1)S(1)}, u32[]{:S(2)}, u32[]{:S(2)}) collective-permute-start(bf16[2,1024,128]{2,1,0:T(8,128)(2,1)} %refs_0_.1), channel_id=1, source_target_pairs={{0,4},{1,13},{2,6},{3,15},{4,8},{5,1},{6,10},{7,3},{8,12},{9,5},{1... | collective-permute-start | bytes 1572872 | tf_op jit(solution)/shard_map/ppermute | solution.py:69
  2.0 2.1 %collective-permute-start.3 = (bf16[2,1024,128]{2,1,0:T(8,128)(2,1)}, bf16[2,1024,128]{2,1,0:T(8,128)(2,1)S(1)}, u32[]{:S(2)}, u32[]{:S(2)}) collective-permute-start(bf16[2,1024,128]{2,1,0:T(8,128)(2,1)} %refs_0_.1), channel_id=1, source_target_pairs={{0,12},{1,5},{2,14},{3,7},{4,0},{5,9},{6,2},{7,11},{8,4},{9,13},{1... | collective-permute-start | bytes 1572872 | tf_op jit(solution)/shard_map/ppermute | solution.py:69
  4.1 3.0 %collective-permute-start.1 = (bf16[2,1024,128]{2,1,0:T(8,128)(2,1)}, bf16[2,1024,128]{2,1,0:T(8,128)(2,1)S(1)}, u32[]{:S(2)}, u32[]{:S(2)}) collective-permute-start(bf16[2,1024,128]{2,1,0:T(8,128)(2,1)} %refs_0_.1), channel_id=1, source_target_pairs={{0,2},{1,3},{2,0},{3,1},{4,6},{5,7},{6,4},{7,5},{8,10},{9,11},{10,... | collective-permute-start | bytes 1572872 | tf_op jit(solution)/shard_map/ppermute | solution.py:69
  7.1 3.2 %collective-permute-start = (bf16[2,1024,128]{2,1,0:T(8,128)(2,1)}, bf16[2,1024,128]{2,1,0:T(8,128)(2,1)S(1)}, u32[]{:S(2)}, u32[]{:S(2)}) collective-permute-start(bf16[2,1024,128]{2,1,0:T(8,128)(2,1)} %refs_0_.1), channel_id=1, source_target_pairs={{0,32},{1,0},{2,80},{3,112},{4,16},{5,48},{6,64},{7,96},{8,33},{9,... | collective-permute-start | bytes 1572872 | tf_op jit(solution)/shard_map/ppermute | solution.py:69
  10.3 0.0 collective-permute-start.4
  10.3 0.9 select_reduce_fusion.1
  11.2 0.1 copy.10
  11.3 0.1 sub.32
  11.4 0.9 select_reduce_fusion
  12.4 1.4 %copy.11.w_ref = f32[2,1024,16]{2,1,0:T(8,128)} copy(f32[2,1024,16]{1,2,0:T(8,128)S(1)} %pad_maximum_fusion) | data formatting | bytes 262144 | tf_op jit(solution)/shard_map/stack | solution.py:91
  13.7 2.2 %shard_map.55.refs_9_ = f32[2,1024,16]{2,1,0:T(8,128)} custom-call(f32[2,1024,16]{2,1,0:T(8,128)} %copy.11.w_ref), custom_call_target="tpu_custom_call" | custom-call | tf_op jit(solution)/shard_map/pallas_call | solution.py:107
  16.0 3.3 %collective-permute-done.2.refs_1_ = bf16[2,1024,128]{2,1,0:T(8,128)(2,1)S(1)} collective-permute-done((bf16[2,1024,128]{2,1,0:T(8,128)(2,1)}, bf16[2,1024,128]{2,1,0:T(8,128)(2,1)S(1)}, u32[]{:S(2)}, u32[]{:S(2)}) %collective-permute-start.2) | collective-permute-done | bytes 524320 | tf_op jit(solution)/shard_map/ppermute | solution.py:69
  19.2 1.1 collective-permute-start.5
  20.4 0.0 collective-permute-start.6
  20.4 0.0 collective-permute-done.1.refs_3_
  20.4 0.5 collective-permute-start.7
  20.9 0.0 collective-permute-done.refs_0_
  20.9 0.0 collective-permute-done.4.refs_0_
  20.9 1.0 collective-permute-done.5.refs_1_
  21.9 0.7 collective-permute-done.6.refs_2_
  22.7 0.7 collective-permute-done.7.refs_3_
  23.4 2.1 %collective-permute-start.15 = (bf16[2,1024,128]{2,1,0:T(8,128)(2,1)S(1)}, bf16[2,1024,128]{2,1,0:T(8,128)(2,1)S(1)}, u32[]{:S(2)}, u32[]{:S(2)}) collective-permute-start(bf16[2,1024,128]{2,1,0:T(8,128)(2,1)S(1)} %collective-permute-done.2.refs_1_), channel_id=1, source_target_pairs={{0,4},{1,13},{2,6},{3,15},{4,8},{5,1},{6,10},{7,3},{8,12},{9,5},{1... | collective-permute-start | bytes 1572872 | tf_op jit(solution)/shard_map/ppermute | solution.py:69
  25.5 3.3 %collective-permute-start.10 = (bf16[2,1024,128]{2,1,0:T(8,128)(2,1)S(1)}, bf16[2,1024,128]{2,1,0:T(8,128)(2,1)S(1)}, u32[]{:S(2)}, u32[]{:S(2)}) collective-permute-start(bf16[2,1024,128]{2,1,0:T(8,128)(2,1)S(1)} %collective-permute-done.refs_0_), channel_id=1, source_target_pairs={{0,32},{1,33},{2,34},{3,35},{4,36},{5,37},{6,38},{7,39},{8,40},{9,... | collective-permute-start | bytes 1572872 | tf_op jit(solution)/shard_map/ppermute | solution.py:69
  28.8 7.3 %collective-permute-start.11 = (bf16[2,1024,128]{2,1,0:T(8,128)(2,1)S(1)}, bf16[2,1024,128]{2,1,0:T(8,128)(2,1)S(1)}, u32[]{:S(2)}, u32[]{:S(2)}) collective-permute-start(bf16[2,1024,128]{2,1,0:T(8,128)(2,1)S(1)} %collective-permute-done.refs_0_), channel_id=1, source_target_pairs={{0,64},{1,65},{2,66},{3,67},{4,68},{5,69},{6,70},{7,71},{8,72},{9,... | collective-permute-start | bytes 1572872 | tf_op jit(solution)/shard_map/ppermute | solution.py:69
  36.1 0.0 collective-permute-start.8
  36.1 1.0 copy-done.1
  37.1 5.8 %shard_map.56.refs_5_ = f32[2,1024,1024]{2,1,0:T(8,128)S(1)} custom-call(bf16[2,1024,128]{2,1,0:T(8,128)(2,1)S(1)} %copy-done.1, bf16[2,1024,128]{2,1,0:T(8,128)(2,1)S(1)} %collective-permute-done.2.refs_1_, bf16[2,1024,128]{2,1,0:T(8,128)(2,1)S(1)} %collective-permute-done.3.refs_2_, bf16[2,1024,128]{2,1,0:T(8,128)(2,1)S(1)} %collective-permute-done.1.refs_3_, ...), custom_call_target="tpu_custom_call" | custom-call | flops 1 | bytes 1 | tf_op jit(solution)/shard_map/pallas_call | solution.py:179
  42.9 0.0 collective-permute-done.15.refs_0_
  42.9 4.1 %collective-permute-start.19 = (bf16[2,1024,128]{2,1,0:T(8,128)(2,1)S(1)}, bf16[2,1024,128]{2,1,0:T(8,128)(2,1)S(1)}, u32[]{:S(2)}, u32[]{:S(2)}) collective-permute-start(bf16[2,1024,128]{2,1,0:T(8,128)(2,1)S(1)} %collective-permute-done.15.refs_0_), channel_id=1, source_target_pairs={{0,2},{1,3},{2,0},{3,1},{4,6},{5,7},{6,4},{7,5},{8,10},{9,11},{10,... | collective-permute-start | bytes 1572872 | tf_op jit(solution)/shard_map/ppermute | solution.py:69
  47.1 3.2 %collective-permute-start.9 = (bf16[2,1024,128]{2,1,0:T(8,128)(2,1)S(1)}, bf16[2,1024,128]{2,1,0:T(8,128)(2,1)S(1)}, u32[]{:S(2)}, u32[]{:S(2)}) collective-permute-start(bf16[2,1024,128]{2,1,0:T(8,128)(2,1)S(1)} %collective-permute-done.refs_0_), channel_id=1, source_target_pairs={{0,48},{1,17},{2,50},{3,19},{4,52},{5,21},{6,54},{7,23},{8,56},{9,... | collective-permute-start | bytes 1572872 | tf_op jit(solution)/shard_map/ppermute | solution.py:69
  50.3 0.1 collective-permute-start.17
  50.4 3.1 %collective-permute-start.21 = (bf16[2,1024,128]{2,1,0:T(8,128)(2,1)S(1)}, bf16[2,1024,128]{2,1,0:T(8,128)(2,1)S(1)}, u32[]{:S(2)}, u32[]{:S(2)}) collective-permute-start(bf16[2,1024,128]{2,1,0:T(8,128)(2,1)S(1)} %collective-permute-done.1.refs_3_), channel_id=1, source_target_pairs={{0,12},{1,5},{2,14},{3,7},{4,0},{5,9},{6,2},{7,11},{8,4},{9,13},{1... | collective-permute-start | bytes 1572872 | tf_op jit(solution)/shard_map/ppermute | solution.py:69
  53.5 0.1 collective-permute-start.16
  53.7 8.4 %collective-permute-done.19.refs_2_ = bf16[2,1024,128]{2,1,0:T(8,128)(2,1)S(1)} collective-permute-done((bf16[2,1024,128]{2,1,0:T(8,128)(2,1)S(1)}, bf16[2,1024,128]{2,1,0:T(8,128)(2,1)S(1)}, u32[]{:S(2)}, u32[]{:S(2)}) %collective-permute-start.19) | collective-permute-done | bytes 524320 | tf_op jit(solution)/shard_map/ppermute | solution.py:69
  62.1 0.9 collective-permute-start.12
  63.0 2.9 %collective-permute-done.17.refs_1_ = bf16[2,1024,128]{2,1,0:T(8,128)(2,1)S(1)} collective-permute-done((bf16[2,1024,128]{2,1,0:T(8,128)(2,1)S(1)}, bf16[2,1024,128]{2,1,0:T(8,128)(2,1)S(1)}, u32[]{:S(2)}, u32[]{:S(2)}) %collective-permute-start.17) | collective-permute-done | bytes 524320 | tf_op jit(solution)/shard_map/ppermute | solution.py:69
  66.0 0.0 collective-permute-done.21.refs_3_
  66.0 0.5 collective-permute-start.22
  66.5 0.0 collective-permute-done.16.refs_0_
  66.5 0.0 collective-permute-start.13
  66.5 0.0 collective-permute-done.20.refs_2_
  66.5 0.6 collective-permute-start.14
  67.0 5.8 %shard_map.57.refs_5_ = f32[2,1024,1024]{2,1,0:T(8,128)S(1)} custom-call(bf16[2,1024,128]{2,1,0:T(8,128)(2,1)S(1)} %collective-permute-done.4.refs_0_, bf16[2,1024,128]{2,1,0:T(8,128)(2,1)S(1)} %collective-permute-done.5.refs_1_, bf16[2,1024,128]{2,1,0:T(8,128)(2,1)S(1)} %collective-permute-done.6.refs_2_, ...), custom_call_target="tpu_custom_call", output_to_operand_aliasing={{}: (5, {})} | custom-call | flops 1 | bytes 1 | tf_op jit(solution)/shard_map/pallas_call | solution.py:179
  72.8 5.8 %shard_map.58.refs_5_ = f32[2,1024,1024]{2,1,0:T(8,128)S(1)} custom-call(bf16[2,1024,128]{2,1,0:T(8,128)(2,1)S(1)} %collective-permute-done.15.refs_0_, bf16[2,1024,128]{2,1,0:T(8,128)(2,1)S(1)} %collective-permute-done.17.refs_1_, bf16[2,1024,128]{2,1,0:T(8,128)(2,1)S(1)} %collective-permute-done.19.refs_2_, ...), custom_call_target="tpu_custom_call", output_to_operand_aliasing={{}: (5, {})} | custom-call | flops 1 | bytes 1 | tf_op jit(solution)/shard_map/pallas_call | solution.py:179
  78.6 0.0 collective-permute-done.18.refs_1_
  78.6 5.9 %shard_map.59.refs_8_ = f32[2,1024,1024]{2,1,0:T(8,128)S(1)} custom-call(bf16[2,1024,128]{2,1,0:T(8,128)(2,1)S(1)} %collective-permute-done.16.refs_0_, bf16[2,1024,128]{2,1,0:T(8,128)(2,1)S(1)} %collective-permute-done.18.refs_1_, bf16[2,1024,128]{2,1,0:T(8,128)(2,1)S(1)} %collective-permute-done.20.refs_2_, ...), custom_call_target="tpu_custom_call", output_to_operand_aliasing={{}: (5, {})} | custom-call | flops 1 | bytes 1 | tf_op jit(solution)/shard_map/pallas_call | solution.py:179
  84.5 0.0 collective-permute-done.12.refs_5_
  84.5 0.0 collective-permute-done.13.refs_6_
  84.6 2.6 %shard_map.60 = f32[2,4,16]{2,1,0:T(4,128)S(1)} custom-call(bf16[2,1024,128]{2,1,0:T(8,128)(2,1)S(1)} %collective-permute-done.refs_0_, bf16[2,1024,128]{2,1,0:T(8,128)(2,1)S(1)} %collective-permute-done.8.refs_1_, bf16[2,1024,128]{2,1,0:T(8,128)(2,1)S(1)} %collective-permute-done.10.refs_2_, bf16[2,1024,128]{2,1,0:T(8,128)(2,1)S(1)} %collective-permute-done.9.refs_3_, ...), custom_call_target="tpu_custom_call" | custom-call | flops 1 | bytes 1 | tf_op jit(solution)/shard_map/pallas_call | solution.py:239
  87.1 0.1 collective-permute-start.23
  87.2 1.2 %collective-permute-done.23 = f32[2,4,16]{2,1,0:T(4,128)S(1)} collective-permute-done((f32[2,4,16]{2,1,0:T(4,128)S(1)}, f32[2,4,16]{2,1,0:T(4,128)S(1)}, u32[]{:S(2)}, u32[]{:S(2)}) %collective-permute-start.23) | collective-permute-done | bytes 544 | tf_op jit(solution)/shard_map/ppermute | solution.py:69
  88.4 1.7 %collective-permute-start.24 = (f32[2,4,16]{2,1,0:T(4,128)S(1)}, f32[2,4,16]{2,1,0:T(4,128)S(1)}, u32[]{:S(2)}, u32[]{:S(2)}) collective-permute-start(f32[2,4,16]{2,1,0:T(4,128)S(1)} %add.42), channel_id=1, source_target_pairs={{0,64},{1,65},{2,66},{3,67},{4,68},{5,69},{6,70},{7,71},{8,72},{9,... | collective-permute-start | bytes 1544 | tf_op jit(solution)/shard_map/ppermute | solution.py:69
  90.1 1.9 %collective-permute-done.24 = f32[2,4,16]{2,1,0:T(4,128)S(1)} collective-permute-done((f32[2,4,16]{2,1,0:T(4,128)S(1)}, f32[2,4,16]{2,1,0:T(4,128)S(1)}, u32[]{:S(2)}, u32[]{:S(2)}) %collective-permute-start.24) | collective-permute-done | bytes 544 | tf_op jit(solution)/shard_map/ppermute | solution.py:69
  92.0 1.9 %collective-permute-start.25 = (f32[2,4,16]{2,1,0:T(4,128)S(1)}, f32[2,4,16]{2,1,0:T(4,128)S(1)}, u32[]{:S(2)}, u32[]{:S(2)}) collective-permute-start(f32[2,4,16]{2,1,0:T(4,128)S(1)} %add.43), channel_id=1, source_target_pairs={{0,66},{1,67},{2,64},{3,65},{4,70},{5,71},{6,68},{7,69},{8,74},{9,... | collective-permute-start | bytes 1544 | tf_op jit(solution)/shard_map/ppermute | solution.py:69
  93.8 2.9 %collective-permute-done.25 = f32[2,4,16]{2,1,0:T(4,128)S(1)} collective-permute-done((f32[2,4,16]{2,1,0:T(4,128)S(1)}, f32[2,4,16]{2,1,0:T(4,128)S(1)}, u32[]{:S(2)}, u32[]{:S(2)}) %collective-permute-start.25) | collective-permute-done | bytes 544 | tf_op jit(solution)/shard_map/ppermute | solution.py:69
  96.8 1.5 %collective-permute-start.26 = (f32[2,4,16]{2,1,0:T(4,128)S(1)}, f32[2,4,16]{2,1,0:T(4,128)S(1)}, u32[]{:S(2)}, u32[]{:S(2)}) collective-permute-start(f32[2,4,16]{2,1,0:T(4,128)S(1)} %add.44), channel_id=1, source_target_pairs={{0,16},{1,17},{2,18},{3,19},{4,20},{5,21},{6,22},{7,23},{8,24},{9,... | collective-permute-start | bytes 1544 | tf_op jit(solution)/shard_map/ppermute | solution.py:69
  98.3 2.1 %collective-permute-done.26 = f32[2,4,16]{2,1,0:T(4,128)S(1)} collective-permute-done((f32[2,4,16]{2,1,0:T(4,128)S(1)}, f32[2,4,16]{2,1,0:T(4,128)S(1)}, u32[]{:S(2)}, u32[]{:S(2)}) %collective-permute-start.26) | collective-permute-done | bytes 544 | tf_op jit(solution)/shard_map/ppermute | solution.py:69
  100.4 2.1 %collective-permute-start.27 = (f32[2,4,16]{2,1,0:T(4,128)S(1)}, f32[2,4,16]{2,1,0:T(4,128)S(1)}, u32[]{:S(2)}, u32[]{:S(2)}) collective-permute-start(f32[2,4,16]{2,1,0:T(4,128)S(1)} %add.45), channel_id=1, source_target_pairs={{0,48},{1,49},{2,50},{3,51},{4,52},{5,53},{6,54},{7,55},{8,56},{9,... | collective-permute-start | bytes 1544 | tf_op jit(solution)/shard_map/ppermute | solution.py:69
  102.5 2.7 %collective-permute-done.27 = f32[2,4,16]{2,1,0:T(4,128)S(1)} collective-permute-done((f32[2,4,16]{2,1,0:T(4,128)S(1)}, f32[2,4,16]{2,1,0:T(4,128)S(1)}, u32[]{:S(2)}, u32[]{:S(2)}) %collective-permute-start.27) | collective-permute-done | bytes 544 | tf_op jit(solution)/shard_map/ppermute | solution.py:69
  105.2 0.2 collective-permute-start.28
  105.4 3.4 %collective-permute-done.28 = f32[2,4,16]{2,1,0:T(4,128)S(1)} collective-permute-done((f32[2,4,16]{2,1,0:T(4,128)S(1)}, f32[2,4,16]{2,1,0:T(4,128)S(1)}, u32[]{:S(2)}, u32[]{:S(2)}) %collective-permute-start.28) | collective-permute-done | bytes 544 | tf_op jit(solution)/shard_map/ppermute | solution.py:69
  108.8 1.7 %collective-permute-start.29 = (f32[2,4,16]{2,1,0:T(4,128)S(1)}, f32[2,4,16]{2,1,0:T(4,128)S(1)}, u32[]{:S(2)}, u32[]{:S(2)}) collective-permute-start(f32[2,4,16]{2,1,0:T(4,128)S(1)} %add.47), channel_id=1, source_target_pairs={{0,12},{1,13},{2,14},{3,15},{4,8},{5,9},{6,10},{7,11},{8,4},{9,5},... | collective-permute-start | bytes 1544 | tf_op jit(solution)/shard_map/ppermute | solution.py:69
  110.6 3.1 %collective-permute-done.29 = f32[2,4,16]{2,1,0:T(4,128)S(1)} collective-permute-done((f32[2,4,16]{2,1,0:T(4,128)S(1)}, f32[2,4,16]{2,1,0:T(4,128)S(1)}, u32[]{:S(2)}, u32[]{:S(2)}) %collective-permute-start.29) | collective-permute-done | bytes 544 | tf_op jit(solution)/shard_map/ppermute | solution.py:69
  113.7 0.6 add.48
  (23 shorter events, 0.1 us)
Async XLA Ops:
  0.0 19.2 %collective-permute-start.2 = (bf16[2,1024,128]{2,1,0:T(8,128)(2,1)}, bf16[2,1024,128]{2,1,0:T(8,128)(2,1)S(1)}, u32[]{:S(2)}, u32[]{:S(2)}) collective-permute-start(bf16[2,1024,128]{2,1,0:T(8,128)(2,1)} %refs_0_.1), channel_id=1, source_target_pairs={{0,4},{1,13},{2,6},{3,15},{4,8},{5,1},{6,10},{7,3},{8,12},{9,5},{1... | collective-permute-start | bytes 1572872 | tf_op jit(solution)/shard_map/ppermute | solution.py:69
  2.0 17.2 %collective-permute-start.3 = (bf16[2,1024,128]{2,1,0:T(8,128)(2,1)}, bf16[2,1024,128]{2,1,0:T(8,128)(2,1)S(1)}, u32[]{:S(2)}, u32[]{:S(2)}) collective-permute-start(bf16[2,1024,128]{2,1,0:T(8,128)(2,1)} %refs_0_.1), channel_id=1, source_target_pairs={{0,12},{1,5},{2,14},{3,7},{4,0},{5,9},{6,2},{7,11},{8,4},{9,13},{1... | collective-permute-start | bytes 1572872 | tf_op jit(solution)/shard_map/ppermute | solution.py:69
  4.1 16.3 %collective-permute-start.1 = (bf16[2,1024,128]{2,1,0:T(8,128)(2,1)}, bf16[2,1024,128]{2,1,0:T(8,128)(2,1)S(1)}, u32[]{:S(2)}, u32[]{:S(2)}) collective-permute-start(bf16[2,1024,128]{2,1,0:T(8,128)(2,1)} %refs_0_.1), channel_id=1, source_target_pairs={{0,2},{1,3},{2,0},{3,1},{4,6},{5,7},{6,4},{7,5},{8,10},{9,11},{10,... | collective-permute-start | bytes 1572872 | tf_op jit(solution)/shard_map/ppermute | solution.py:69
  7.1 13.7 %collective-permute-start = (bf16[2,1024,128]{2,1,0:T(8,128)(2,1)}, bf16[2,1024,128]{2,1,0:T(8,128)(2,1)S(1)}, u32[]{:S(2)}, u32[]{:S(2)}) collective-permute-start(bf16[2,1024,128]{2,1,0:T(8,128)(2,1)} %refs_0_.1), channel_id=1, source_target_pairs={{0,32},{1,0},{2,80},{3,112},{4,16},{5,48},{6,64},{7,96},{8,33},{9,... | collective-permute-start | bytes 1572872 | tf_op jit(solution)/shard_map/ppermute | solution.py:69
  10.3 10.5 %collective-permute-start.4 = (bf16[2,1024,128]{2,1,0:T(8,128)(2,1)}, bf16[2,1024,128]{2,1,0:T(8,128)(2,1)S(1)}, u32[]{:S(2)}, u32[]{:S(2)}) collective-permute-start(bf16[2,1024,128]{2,1,0:T(8,128)(2,1)} %refs_0_.1), channel_id=1, source_target_pairs={{0,1},{1,0},{2,3},{3,2},{4,5},{5,4},{6,7},{7,6},{8,9},{9,8},{10,11... | collective-permute-start | bytes 1572872 | tf_op jit(solution)/shard_map/ppermute | solution.py:69
  19.2 2.7 %collective-permute-start.5 = (bf16[2,1024,128]{2,1,0:T(8,128)(2,1)S(1)}, bf16[2,1024,128]{2,1,0:T(8,128)(2,1)S(1)}, u32[]{:S(2)}, u32[]{:S(2)}) collective-permute-start(bf16[2,1024,128]{2,1,0:T(8,128)(2,1)S(1)} %collective-permute-done.2.refs_1_), channel_id=1, source_target_pairs={{0,1},{1,0},{2,3},{3,2},{4,5},{5,4},{6,7},{7,6},{8,9},{9,8},{10,11... | collective-permute-start | bytes 1572872 | tf_op jit(solution)/shard_map/ppermute | solution.py:69
  20.4 2.3 %collective-permute-start.6 = (bf16[2,1024,128]{2,1,0:T(8,128)(2,1)S(1)}, bf16[2,1024,128]{2,1,0:T(8,128)(2,1)S(1)}, u32[]{:S(2)}, u32[]{:S(2)}) collective-permute-start(bf16[2,1024,128]{2,1,0:T(8,128)(2,1)S(1)} %collective-permute-done.3.refs_2_), channel_id=1, source_target_pairs={{0,1},{1,0},{2,3},{3,2},{4,5},{5,4},{6,7},{7,6},{8,9},{9,8},{10,11... | collective-permute-start | bytes 1572872 | tf_op jit(solution)/shard_map/ppermute | solution.py:69
  20.4 3.0 %collective-permute-start.7 = (bf16[2,1024,128]{2,1,0:T(8,128)(2,1)S(1)}, bf16[2,1024,128]{2,1,0:T(8,128)(2,1)S(1)}, u32[]{:S(2)}, u32[]{:S(2)}) collective-permute-start(bf16[2,1024,128]{2,1,0:T(8,128)(2,1)S(1)} %collective-permute-done.1.refs_3_), channel_id=1, source_target_pairs={{0,1},{1,0},{2,3},{3,2},{4,5},{5,4},{6,7},{7,6},{8,9},{9,8},{10,11... | collective-permute-start | bytes 1572872 | tf_op jit(solution)/shard_map/ppermute | solution.py:69
  23.4 19.5 %collective-permute-start.15 = (bf16[2,1024,128]{2,1,0:T(8,128)(2,1)S(1)}, bf16[2,1024,128]{2,1,0:T(8,128)(2,1)S(1)}, u32[]{:S(2)}, u32[]{:S(2)}) collective-permute-start(bf16[2,1024,128]{2,1,0:T(8,128)(2,1)S(1)} %collective-permute-done.2.refs_1_), channel_id=1, source_target_pairs={{0,4},{1,13},{2,6},{3,15},{4,8},{5,1},{6,10},{7,3},{8,12},{9,5},{1... | collective-permute-start | bytes 1572872 | tf_op jit(solution)/shard_map/ppermute | solution.py:69
  25.5 24.8 %collective-permute-start.10 = (bf16[2,1024,128]{2,1,0:T(8,128)(2,1)S(1)}, bf16[2,1024,128]{2,1,0:T(8,128)(2,1)S(1)}, u32[]{:S(2)}, u32[]{:S(2)}) collective-permute-start(bf16[2,1024,128]{2,1,0:T(8,128)(2,1)S(1)} %collective-permute-done.refs_0_), channel_id=1, source_target_pairs={{0,32},{1,33},{2,34},{3,35},{4,36},{5,37},{6,38},{7,39},{8,40},{9,... | collective-permute-start | bytes 1572872 | tf_op jit(solution)/shard_map/ppermute | solution.py:69
  28.8 21.6 %collective-permute-start.11 = (bf16[2,1024,128]{2,1,0:T(8,128)(2,1)S(1)}, bf16[2,1024,128]{2,1,0:T(8,128)(2,1)S(1)}, u32[]{:S(2)}, u32[]{:S(2)}) collective-permute-start(bf16[2,1024,128]{2,1,0:T(8,128)(2,1)S(1)} %collective-permute-done.refs_0_), channel_id=1, source_target_pairs={{0,64},{1,65},{2,66},{3,67},{4,68},{5,69},{6,70},{7,71},{8,72},{9,... | collective-permute-start | bytes 1572872 | tf_op jit(solution)/shard_map/ppermute | solution.py:69
  36.1 17.5 %collective-permute-start.8 = (bf16[2,1024,128]{2,1,0:T(8,128)(2,1)S(1)}, bf16[2,1024,128]{2,1,0:T(8,128)(2,1)S(1)}, u32[]{:S(2)}, u32[]{:S(2)}) collective-permute-start(bf16[2,1024,128]{2,1,0:T(8,128)(2,1)S(1)} %collective-permute-done.refs_0_), channel_id=1, source_target_pairs={{0,16},{1,49},{2,18},{3,51},{4,20},{5,53},{6,22},{7,55},{8,24},{9,... | collective-permute-start | bytes 1572872 | tf_op jit(solution)/shard_map/ppermute | solution.py:69
  36.1 1.0 copy-start.1
  42.9 19.2 %collective-permute-start.19 = (bf16[2,1024,128]{2,1,0:T(8,128)(2,1)S(1)}, bf16[2,1024,128]{2,1,0:T(8,128)(2,1)S(1)}, u32[]{:S(2)}, u32[]{:S(2)}) collective-permute-start(bf16[2,1024,128]{2,1,0:T(8,128)(2,1)S(1)} %collective-permute-done.15.refs_0_), channel_id=1, source_target_pairs={{0,2},{1,3},{2,0},{3,1},{4,6},{5,7},{6,4},{7,5},{8,10},{9,11},{10,... | collective-permute-start | bytes 1572872 | tf_op jit(solution)/shard_map/ppermute | solution.py:69
  47.1 15.0 %collective-permute-start.9 = (bf16[2,1024,128]{2,1,0:T(8,128)(2,1)S(1)}, bf16[2,1024,128]{2,1,0:T(8,128)(2,1)S(1)}, u32[]{:S(2)}, u32[]{:S(2)}) collective-permute-start(bf16[2,1024,128]{2,1,0:T(8,128)(2,1)S(1)} %collective-permute-done.refs_0_), channel_id=1, source_target_pairs={{0,48},{1,17},{2,50},{3,19},{4,52},{5,21},{6,54},{7,23},{8,56},{9,... | collective-permute-start | bytes 1572872 | tf_op jit(solution)/shard_map/ppermute | solution.py:69
  50.3 15.7 %collective-permute-start.17 = (bf16[2,1024,128]{2,1,0:T(8,128)(2,1)S(1)}, bf16[2,1024,128]{2,1,0:T(8,128)(2,1)S(1)}, u32[]{:S(2)}, u32[]{:S(2)}) collective-permute-start(bf16[2,1024,128]{2,1,0:T(8,128)(2,1)S(1)} %collective-permute-done.1.refs_3_), channel_id=1, source_target_pairs={{0,4},{1,13},{2,6},{3,15},{4,8},{5,1},{6,10},{7,3},{8,12},{9,5},{1... | collective-permute-start | bytes 1572872 | tf_op jit(solution)/shard_map/ppermute | solution.py:69
  50.4 15.6 %collective-permute-start.21 = (bf16[2,1024,128]{2,1,0:T(8,128)(2,1)S(1)}, bf16[2,1024,128]{2,1,0:T(8,128)(2,1)S(1)}, u32[]{:S(2)}, u32[]{:S(2)}) collective-permute-start(bf16[2,1024,128]{2,1,0:T(8,128)(2,1)S(1)} %collective-permute-done.1.refs_3_), channel_id=1, source_target_pairs={{0,12},{1,5},{2,14},{3,7},{4,0},{5,9},{6,2},{7,11},{8,4},{9,13},{1... | collective-permute-start | bytes 1572872 | tf_op jit(solution)/shard_map/ppermute | solution.py:69
  53.5 12.9 %collective-permute-start.16 = (bf16[2,1024,128]{2,1,0:T(8,128)(2,1)S(1)}, bf16[2,1024,128]{2,1,0:T(8,128)(2,1)S(1)}, u32[]{:S(2)}, u32[]{:S(2)}) collective-permute-start(bf16[2,1024,128]{2,1,0:T(8,128)(2,1)S(1)} %collective-permute-done.15.refs_0_), channel_id=1, source_target_pairs={{0,1},{1,0},{2,3},{3,2},{4,5},{5,4},{6,7},{7,6},{8,9},{9,8},{10,11... | collective-permute-start | bytes 1572872 | tf_op jit(solution)/shard_map/ppermute | solution.py:69
  62.1 4.4 %collective-permute-start.20 = (bf16[2,1024,128]{2,1,0:T(8,128)(2,1)S(1)}, bf16[2,1024,128]{2,1,0:T(8,128)(2,1)S(1)}, u32[]{:S(2)}, u32[]{:S(2)}) collective-permute-start(bf16[2,1024,128]{2,1,0:T(8,128)(2,1)S(1)} %collective-permute-done.19.refs_2_), channel_id=1, source_target_pairs={{0,1},{1,0},{2,3},{3,2},{4,5},{5,4},{6,7},{7,6},{8,9},{9,8},{10,11... | collective-permute-start | bytes 1572872 | tf_op jit(solution)/shard_map/ppermute | solution.py:69
  62.1 22.4 %collective-permute-start.12 = (bf16[2,1024,128]{2,1,0:T(8,128)(2,1)S(1)}, bf16[2,1024,128]{2,1,0:T(8,128)(2,1)S(1)}, u32[]{:S(2)}, u32[]{:S(2)}) collective-permute-start(bf16[2,1024,128]{2,1,0:T(8,128)(2,1)S(1)} %collective-permute-done.11.refs_4_), channel_id=1, source_target_pairs={{0,16},{1,49},{2,18},{3,51},{4,20},{5,53},{6,22},{7,55},{8,24},{9,... | collective-permute-start | bytes 1572872 | tf_op jit(solution)/shard_map/ppermute | solution.py:69
  65.9 12.7 %collective-permute-start.18 = (bf16[2,1024,128]{2,1,0:T(8,128)(2,1)S(1)}, bf16[2,1024,128]{2,1,0:T(8,128)(2,1)S(1)}, u32[]{:S(2)}, u32[]{:S(2)}) collective-permute-start(bf16[2,1024,128]{2,1,0:T(8,128)(2,1)S(1)} %collective-permute-done.17.refs_1_), channel_id=1, source_target_pairs={{0,1},{1,0},{2,3},{3,2},{4,5},{5,4},{6,7},{7,6},{8,9},{9,8},{10,11... | collective-permute-start | bytes 1572872 | tf_op jit(solution)/shard_map/ppermute | solution.py:69
  66.0 12.7 %collective-permute-start.22 = (bf16[2,1024,128]{2,1,0:T(8,128)(2,1)S(1)}, bf16[2,1024,128]{2,1,0:T(8,128)(2,1)S(1)}, u32[]{:S(2)}, u32[]{:S(2)}) collective-permute-start(bf16[2,1024,128]{2,1,0:T(8,128)(2,1)S(1)} %collective-permute-done.21.refs_3_), channel_id=1, source_target_pairs={{0,1},{1,0},{2,3},{3,2},{4,5},{5,4},{6,7},{7,6},{8,9},{9,8},{10,11... | collective-permute-start | bytes 1572872 | tf_op jit(solution)/shard_map/ppermute | solution.py:69
  66.5 18.1 %collective-permute-start.13 = (bf16[2,1024,128]{2,1,0:T(8,128)(2,1)S(1)}, bf16[2,1024,128]{2,1,0:T(8,128)(2,1)S(1)}, u32[]{:S(2)}, u32[]{:S(2)}) collective-permute-start(bf16[2,1024,128]{2,1,0:T(8,128)(2,1)S(1)} %collective-permute-done.11.refs_4_), channel_id=1, source_target_pairs={{0,48},{1,17},{2,50},{3,19},{4,52},{5,21},{6,54},{7,23},{8,56},{9,... | collective-permute-start | bytes 1572872 | tf_op jit(solution)/shard_map/ppermute | solution.py:69
  66.5 18.1 %collective-permute-start.14 = (bf16[2,1024,128]{2,1,0:T(8,128)(2,1)S(1)}, bf16[2,1024,128]{2,1,0:T(8,128)(2,1)S(1)}, u32[]{:S(2)}, u32[]{:S(2)}) collective-permute-start(bf16[2,1024,128]{2,1,0:T(8,128)(2,1)S(1)} %collective-permute-done.10.refs_2_), channel_id=1, source_target_pairs={{0,64},{1,65},{2,66},{3,67},{4,68},{5,69},{6,70},{7,71},{8,72},{9,... | collective-permute-start | bytes 1572872 | tf_op jit(solution)/shard_map/ppermute | solution.py:69
  78.6 5.9 %copy-start = (f32[2,1024,16]{2,1,0:T(8,128)S(1)}, f32[2,1024,16]{2,1,0:T(8,128)}, u32[]{:S(2)}) copy-start(f32[2,1024,16]{2,1,0:T(8,128)} %shard_map.55.refs_9_) | copy-start | bytes 393220
  87.1 1.2 %collective-permute-start.23 = (f32[2,4,16]{2,1,0:T(4,128)S(1)}, f32[2,4,16]{2,1,0:T(4,128)S(1)}, u32[]{:S(2)}, u32[]{:S(2)}) collective-permute-start(f32[2,4,16]{2,1,0:T(4,128)S(1)} %shard_map.60), channel_id=1, source_target_pairs={{0,1},{1,0},{2,3},{3,2},{4,5},{5,4},{6,7},{7,6},{8,9},{9,8},{10,11... | collective-permute-start | bytes 1544 | tf_op jit(solution)/shard_map/ppermute | solution.py:69
  88.4 3.6 %collective-permute-start.24 = (f32[2,4,16]{2,1,0:T(4,128)S(1)}, f32[2,4,16]{2,1,0:T(4,128)S(1)}, u32[]{:S(2)}, u32[]{:S(2)}) collective-permute-start(f32[2,4,16]{2,1,0:T(4,128)S(1)} %add.42), channel_id=1, source_target_pairs={{0,64},{1,65},{2,66},{3,67},{4,68},{5,69},{6,70},{7,71},{8,72},{9,... | collective-permute-start | bytes 1544 | tf_op jit(solution)/shard_map/ppermute | solution.py:69
  92.0 4.8 %collective-permute-start.25 = (f32[2,4,16]{2,1,0:T(4,128)S(1)}, f32[2,4,16]{2,1,0:T(4,128)S(1)}, u32[]{:S(2)}, u32[]{:S(2)}) collective-permute-start(f32[2,4,16]{2,1,0:T(4,128)S(1)} %add.43), channel_id=1, source_target_pairs={{0,66},{1,67},{2,64},{3,65},{4,70},{5,71},{6,68},{7,69},{8,74},{9,... | collective-permute-start | bytes 1544 | tf_op jit(solution)/shard_map/ppermute | solution.py:69
  96.8 3.6 %collective-permute-start.26 = (f32[2,4,16]{2,1,0:T(4,128)S(1)}, f32[2,4,16]{2,1,0:T(4,128)S(1)}, u32[]{:S(2)}, u32[]{:S(2)}) collective-permute-start(f32[2,4,16]{2,1,0:T(4,128)S(1)} %add.44), channel_id=1, source_target_pairs={{0,16},{1,17},{2,18},{3,19},{4,20},{5,21},{6,22},{7,23},{8,24},{9,... | collective-permute-start | bytes 1544 | tf_op jit(solution)/shard_map/ppermute | solution.py:69
  100.4 4.8 %collective-permute-start.27 = (f32[2,4,16]{2,1,0:T(4,128)S(1)}, f32[2,4,16]{2,1,0:T(4,128)S(1)}, u32[]{:S(2)}, u32[]{:S(2)}) collective-permute-start(f32[2,4,16]{2,1,0:T(4,128)S(1)} %add.45), channel_id=1, source_target_pairs={{0,48},{1,49},{2,50},{3,51},{4,52},{5,53},{6,54},{7,55},{8,56},{9,... | collective-permute-start | bytes 1544 | tf_op jit(solution)/shard_map/ppermute | solution.py:69
  105.2 3.6 %collective-permute-start.28 = (f32[2,4,16]{2,1,0:T(4,128)S(1)}, f32[2,4,16]{2,1,0:T(4,128)S(1)}, u32[]{:S(2)}, u32[]{:S(2)}) collective-permute-start(f32[2,4,16]{2,1,0:T(4,128)S(1)} %add.46), channel_id=1, source_target_pairs={{0,4},{1,5},{2,6},{3,7},{4,0},{5,1},{6,2},{7,3},{8,12},{9,13},{10,... | collective-permute-start | bytes 1544 | tf_op jit(solution)/shard_map/ppermute | solution.py:69
  108.8 4.8 %collective-permute-start.29 = (f32[2,4,16]{2,1,0:T(4,128)S(1)}, f32[2,4,16]{2,1,0:T(4,128)S(1)}, u32[]{:S(2)}, u32[]{:S(2)}) collective-permute-start(f32[2,4,16]{2,1,0:T(4,128)S(1)} %add.47), channel_id=1, source_target_pairs={{0,12},{1,13},{2,14},{3,15},{4,8},{5,9},{6,10},{7,11},{8,4},{9,5},... | collective-permute-start | bytes 1544 | tf_op jit(solution)/shard_map/ppermute | solution.py:69
